TPU v7x, 32 devices: a whole 2x2x4 slice. The times are simulated.
32 devices in a mesh: dp: 8 (over z, y), tensor: 4 (over x, core).
Axes of the slice: x: 2, y: 2, z: 4, core: 2. Of those that a mesh axis runs over, the one named last changes fastest.
Arguments:
- tokens: bfloat16 [16384, 768], P(('dp', 'tensor')), may hold values from -6 to 6
- lengths: int32 [8], P('dp'), may hold values from 512 to 2048, as said below
- arrival_slots: int32 [8, 2048], P('dp'), may hold values from 0 to 2047, each once within a row
- w_qkv: float32 [3, 768, 768], P(None, 'dp', 'tensor'), may hold values from -0.21875 to 0.21875
- w_out: float32 [768, 768], P('tensor', 'dp'), may hold values from -1.75 to 1.75
- w_up: float32 [768, 3072], P('dp', 'tensor'), may hold values from -0.21875 to 0.21875
- w_down: float32 [3072, 768], P('tensor', 'dp'), may hold values from -0.109375 to 0.109375
- w_proj: float32 [768, 128], P('dp'), may hold values from -0.21875 to 0.21875
- norm_gains: float32 [2, 768], P(None, 'dp'), may hold values from 0.1 to 1.9
- biases: float32 [6, 768], P(None, 'dp'), may hold values from -4 to 4
- up_bias: float32 [3072], P('dp'), may hold values from -4 to 4
- cotangent: bfloat16 [16384, 128], P(('dp', 'tensor')), may hold values from -6 to 6
Outputs:
- embeddings: float32 [16384, 128], P(('dp', 'tensor'))
- grad_tokens: float32 [16384, 768], P(('dp', 'tensor'))
- grad_qkv: float32 [3, 768, 768], P(None, 'dp', 'tensor')
- grad_out: float32 [768, 768], P('tensor', 'dp')
- grad_up: float32 [768, 3072], P('dp', 'tensor')
- grad_down: float32 [3072, 768], P('tensor', 'dp')
- grad_proj: float32 [768, 128], P('dp')
- grad_gains: float32 [2, 768], P(None, 'dp')
- grad_biases: float32 [6, 768], P(None, 'dp')
- grad_up_bias: float32 [3072], P('dp')
Inputs may be any that keep to these rules, and one draw needn't show every extreme that they name: `lengths`: some passage fills its whole slot of 2048 positions. `arrival_slots`: each row names every slot of its group once.
All inputs are finite; a program needn't handle non-finite values.
Results may differ from a plain program's by a relative error of at most 0.02.
Values may be sent and summed in bfloat16 or wider, within the bound.
A program may use at most 128 MiB of HBM per device.

v0:
```python
import jax
import jax.numpy as jnp
from jax import lax
from jax.sharding import PartitionSpec as P

HEAD_DIM = 64
SLOT = 2048


EPS_NORM = 1e-06
EPS_UNIT = 1e-06
NEG_FILL = -1e30


def norm_rows(values, gain, shift):
    center = values - jnp.mean(values, axis=-1, keepdims=True)
    spread = jnp.mean(center * center, axis=-1, keepdims=True)
    return center * lax.rsqrt(spread + EPS_NORM) * gain + shift


def gelu_exact(values):
    return jax.nn.gelu(values, approximate=False)


def contract_rows(left, right):
    return lax.dot_general(
        left, right, (((0,), (0,)), ((), ())), preferred_element_type=jnp.float32
    )


def times_transposed(left, right):
    return lax.dot_general(
        left, right, (((1,), (1,)), ((), ())), preferred_element_type=jnp.float32
    )


def attend(query_heads, key_heads, value_heads, key_mask, num_blocks, factor):

    def one_block(position):
        passage_idx = position // num_blocks
        block_idx = position % num_blocks
        query_block = query_heads[passage_idx, block_idx]
        scores = (
            jnp.einsum(
                "qhe,khe->hqk",
                query_block,
                key_heads[passage_idx],
                preferred_element_type=jnp.float32,
            )
            * factor
        )
        scores = jnp.where(key_mask[passage_idx][None, None, :], scores, NEG_FILL)
        row_top = jnp.max(scores, axis=-1, keepdims=True)
        shifted = jnp.exp(scores - row_top)
        row_total = jnp.sum(shifted, axis=-1, keepdims=True)
        soft_low = (shifted / row_total).astype(jnp.bfloat16)
        result = jnp.einsum(
            "hqk,khe->qhe", soft_low, value_heads[passage_idx], preferred_element_type=jnp.float32
        )
        return (result, (row_top + jnp.log(row_total))[..., 0])

    return lax.map(one_block, jnp.arange(query_heads.shape[0] * num_blocks))


def attend_back(
    query_heads, key_heads, value_heads, dcontext_heads, log_total, key_mask, num_blocks, factor
):

    def passage(passage_idx):
        key_rows = key_heads[passage_idx]
        value_rows = value_heads[passage_idx]
        mask_row = key_mask[passage_idx][None, None, :]

        def step(carry, block_idx):
            dkey_sum, dvalue_sum = carry
            query_block = query_heads[passage_idx, block_idx]
            dout_block = dcontext_heads[passage_idx, block_idx]
            total_block = log_total[passage_idx * num_blocks + block_idx]
            scores = (
                jnp.einsum(
                    "qhe,khe->hqk", query_block, key_rows, preferred_element_type=jnp.float32
                )
                * factor
            )
            scores = jnp.where(mask_row, scores, NEG_FILL)
            soft_probs = jnp.exp(scores - total_block[..., None])
            dvalue_sum = dvalue_sum + jnp.einsum(
                "hqk,qhe->khe",
                soft_probs.astype(jnp.bfloat16),
                dout_block,
                preferred_element_type=jnp.float32,
            )
            dsoft = jnp.einsum(
                "qhe,khe->hqk", dout_block, value_rows, preferred_element_type=jnp.float32
            )
            dscore = (
                soft_probs * (dsoft - jnp.sum(soft_probs * dsoft, axis=-1, keepdims=True))
            ).astype(jnp.bfloat16)
            dquery = (
                jnp.einsum("hqk,khe->qhe", dscore, key_rows, preferred_element_type=jnp.float32)
                * factor
            )
            dkey_sum = (
                dkey_sum
                + jnp.einsum(
                    "hqk,qhe->khe", dscore, query_block, preferred_element_type=jnp.float32
                )
                * factor
            )
            return ((dkey_sum, dvalue_sum), dquery)

        zero_grad = jnp.zeros(key_rows.shape, jnp.float32)
        (dkey_sum, dvalue_sum), dquery = lax.scan(
            step, (zero_grad, zero_grad), jnp.arange(num_blocks)
        )
        return (dquery, dkey_sum, dvalue_sum)

    return lax.map(passage, jnp.arange(key_heads.shape[0]))


def body(
    tokens,
    lengths,
    arrival_slots,
    w_qkv,
    w_out,
    w_up,
    w_down,
    w_proj,
    norm_gains,
    biases,
    up_bias,
    cotangent,
):
    tensor_size = lax.axis_size("tensor")
    tensor_pos = lax.axis_index("tensor")
    own_rows = tokens.shape[0]
    group_rows = own_rows * tensor_size
    passages = group_rows // SLOT
    block_rows = min(512, SLOT)
    num_blocks = SLOT // block_rows
    factor = HEAD_DIM ** (-0.5)
    slot_order = arrival_slots[0]
    gathered = (
        lax.all_gather(w_qkv.astype(jnp.bfloat16), "dp", axis=1, tiled=True),
        lax.all_gather(w_out.astype(jnp.bfloat16), "dp", axis=1, tiled=True),
        lax.all_gather(w_up.astype(jnp.bfloat16), "dp", axis=0, tiled=True),
        lax.all_gather(w_down.astype(jnp.bfloat16), "dp", axis=1, tiled=True),
        lax.all_gather(w_proj.astype(jnp.bfloat16), "dp", axis=0, tiled=True),
        lax.all_gather(norm_gains.astype(jnp.bfloat16), "dp", axis=1, tiled=True),
        lax.all_gather(biases.astype(jnp.bfloat16), "dp", axis=1, tiled=True),
        lax.all_gather(up_bias.astype(jnp.bfloat16), "dp", axis=0, tiled=True),
    )
    qkv_weight, out_weight, up_weight, down_weight, proj_weight, gain_low, bias_low, upbias_low = (
        gathered
    )
    width_local = qkv_weight.shape[2]
    hidden_local = up_weight.shape[1]
    heads_local = width_local // HEAD_DIM
    gain_full = gain_low.astype(jnp.float32)
    bias_full = bias_low.astype(jnp.float32)
    upbias_full = upbias_low.astype(jnp.float32)
    col_start = tensor_pos * width_local
    query_bias = lax.dynamic_slice_in_dim(bias_full[0], col_start, width_local)
    value_bias = lax.dynamic_slice_in_dim(bias_full[1], col_start, width_local)
    arrived = lax.all_gather(tokens, "tensor", axis=0, tiled=True)
    inverse = (
        jnp.zeros((group_rows,), jnp.int32)
        .at[slot_order]
        .set(jnp.arange(group_rows, dtype=jnp.int32))
    )
    slotted = jnp.take(arrived, inverse, axis=0)
    row_start = tensor_pos * own_rows
    resid_input = lax.dynamic_slice_in_dim(slotted, row_start, own_rows, 0).astype(jnp.float32)
    positions = row_start + jnp.arange(own_rows, dtype=jnp.int32)
    row_keep = (positions % SLOT < lengths[positions // SLOT]).astype(jnp.float32)
    key_mask = jnp.arange(SLOT, dtype=jnp.int32)[None, :] < lengths[:, None]
    qkv_bias = jnp.stack([query_bias, jnp.zeros_like(query_bias), value_bias])
    qkv_all = (
        jnp.einsum("gd,cde->cge", slotted, qkv_weight, preferred_element_type=jnp.float32)
        + qkv_bias[:, None, :]
    ).astype(jnp.bfloat16)
    block_shape = (passages, num_blocks, block_rows, heads_local, HEAD_DIM)
    slot_shape = (passages, SLOT, heads_local, HEAD_DIM)
    query_heads = qkv_all[0].reshape(block_shape)
    key_heads = qkv_all[1].reshape(slot_shape)
    value_heads = qkv_all[2].reshape(slot_shape)
    attended, log_total = attend(query_heads, key_heads, value_heads, key_mask, num_blocks, factor)
    context = attended.reshape(group_rows, width_local).astype(jnp.bfloat16)
    attn_part = lax.psum_scatter(
        jnp.dot(context, out_weight, preferred_element_type=jnp.float32).astype(jnp.bfloat16),
        "tensor",
        scatter_dimension=0,
        tiled=True,
    ).astype(jnp.float32)
    first_sum = resid_input + attn_part + bias_full[2]
    first_norm, back_first = jax.vjp(norm_rows, first_sum, gain_full[0], bias_full[3])
    first_low = first_norm.astype(jnp.bfloat16)
    mid_rows = lax.all_gather(first_low, "tensor", axis=0, tiled=True)
    upbias_own = lax.dynamic_slice_in_dim(upbias_full, tensor_pos * hidden_local, hidden_local)
    ffn_pre = jnp.dot(mid_rows, up_weight, preferred_element_type=jnp.float32) + upbias_own
    hidden = gelu_exact(ffn_pre).astype(jnp.bfloat16)
    ffn_part = lax.psum_scatter(
        jnp.dot(hidden, down_weight, preferred_element_type=jnp.float32).astype(jnp.bfloat16),
        "tensor",
        scatter_dimension=0,
        tiled=True,
    ).astype(jnp.float32)
    second_sum = first_norm + ffn_part + bias_full[4]
    second_norm, back_second = jax.vjp(norm_rows, second_sum, gain_full[1], bias_full[5])
    second_low = second_norm.astype(jnp.bfloat16)
    projected = jnp.dot(second_low, proj_weight, preferred_element_type=jnp.float32)

    def unit_rows(values):
        return (
            values
            * lax.rsqrt(jnp.sum(values * values, axis=-1, keepdims=True) + EPS_UNIT)
            * row_keep[:, None]
        )

    embeddings, back_unit = jax.vjp(unit_rows, projected)
    (dproj,) = back_unit(cotangent.astype(jnp.float32))
    dproj_low = dproj.astype(jnp.bfloat16)
    grad_proj = contract_rows(second_low, dproj_low)
    dsecond_norm = times_transposed(dproj_low, proj_weight)
    dsecond, grad_gain_two, grad_shift_two = back_second(dsecond_norm)
    dsecond_low = dsecond.astype(jnp.bfloat16)
    dsecond_rows = lax.all_gather(dsecond_low, "tensor", axis=0, tiled=True)
    dhidden = times_transposed(dsecond_rows, down_weight)
    grad_down = contract_rows(hidden, dsecond_rows)
    (dpre,) = jax.vjp(gelu_exact, ffn_pre)[1](dhidden)
    dpre_low = dpre.astype(jnp.bfloat16)
    grad_upbias = lax.dynamic_update_slice_in_dim(
        jnp.zeros(upbias_full.shape, jnp.float32),
        jnp.sum(dpre_low.astype(jnp.float32), axis=0),
        tensor_pos * hidden_local,
        0,
    )
    grad_up = contract_rows(mid_rows, dpre_low)
    dfirst_norm = lax.psum_scatter(
        times_transposed(dpre_low, up_weight).astype(jnp.bfloat16),
        "tensor",
        scatter_dimension=0,
        tiled=True,
    ).astype(jnp.float32)
    dfirst, grad_gain_one, grad_shift_one = back_first(dfirst_norm + dsecond)
    dfirst_low = dfirst.astype(jnp.bfloat16)
    dfirst_rows = lax.all_gather(dfirst_low, "tensor", axis=0, tiled=True)
    dcontext = times_transposed(dfirst_rows, out_weight).astype(jnp.bfloat16)
    grad_out = contract_rows(context, dfirst_rows)
    dquery, dkey, dvalue = attend_back(
        query_heads,
        key_heads,
        value_heads,
        dcontext.reshape(block_shape),
        log_total,
        key_mask,
        num_blocks,
        factor,
    )
    dqkv = jnp.stack(
        [
            dquery.reshape(group_rows, width_local),
            dkey.reshape(group_rows, width_local),
            dvalue.reshape(group_rows, width_local),
        ]
    ).astype(jnp.bfloat16)
    grad_qkv = jnp.einsum("gd,cge->cde", slotted, dqkv, preferred_element_type=jnp.float32)
    column_sums = jnp.sum(dqkv.astype(jnp.float32), axis=1)
    resid_full = lax.dynamic_update_slice_in_dim(
        jnp.zeros((group_rows, dfirst.shape[1]), jnp.float32), dfirst, row_start, 0
    )
    chosen = jnp.take(dqkv, slot_order, axis=1)
    through = jnp.einsum("cge,cde->gd", chosen, qkv_weight, preferred_element_type=jnp.float32)
    grad_tokens = lax.psum_scatter(
        (through + jnp.take(resid_full, slot_order, axis=0)).astype(jnp.bfloat16),
        "tensor",
        scatter_dimension=0,
        tiled=True,
    ).astype(jnp.float32)
    zero_row = jnp.zeros((bias_full.shape[1],), jnp.float32)
    grad_biases = jnp.stack(
        [
            lax.dynamic_update_slice_in_dim(zero_row, column_sums[0], col_start, 0),
            lax.dynamic_update_slice_in_dim(zero_row, column_sums[2], col_start, 0),
            jnp.sum(dfirst, axis=0),
            grad_shift_one,
            jnp.sum(dsecond, axis=0),
            grad_shift_two,
        ]
    )
    grad_gains = jnp.stack([grad_gain_one, grad_gain_two])
    grad_proj, grad_gains, grad_biases, grad_upbias = (
        lax.psum(grad_proj.astype(jnp.bfloat16), "tensor").astype(jnp.float32),
        lax.psum(grad_gains.astype(jnp.bfloat16), "tensor").astype(jnp.float32),
        lax.psum(grad_biases.astype(jnp.bfloat16), "tensor").astype(jnp.float32),
        lax.psum(grad_upbias.astype(jnp.bfloat16), "tensor").astype(jnp.float32),
    )
    summed = (
        lax.psum_scatter(grad_qkv, "dp", scatter_dimension=1, tiled=True),
        lax.psum_scatter(grad_out, "dp", scatter_dimension=1, tiled=True),
        lax.psum_scatter(grad_up, "dp", scatter_dimension=0, tiled=True),
        lax.psum_scatter(grad_down, "dp", scatter_dimension=1, tiled=True),
        lax.psum_scatter(grad_proj, "dp", scatter_dimension=0, tiled=True),
        lax.psum_scatter(grad_gains, "dp", scatter_dimension=1, tiled=True),
        lax.psum_scatter(grad_biases, "dp", scatter_dimension=1, tiled=True),
        lax.psum_scatter(grad_upbias, "dp", scatter_dimension=0, tiled=True),
    )
    return (
        embeddings,
        grad_tokens,
        summed[0],
        summed[1],
        summed[2],
        summed[3],
        summed[4],
        summed[5],
        summed[6],
        summed[7],
    )


def solution(mesh):
    return jax.shard_map(
        body,
        mesh=mesh,
        in_specs=(
            P(("dp", "tensor"), None),
            P("dp"),
            P("dp", None),
            P(None, "dp", "tensor"),
            P("tensor", "dp"),
            P("dp", "tensor"),
            P("tensor", "dp"),
            P("dp", None),
            P(None, "dp"),
            P(None, "dp"),
            P("dp"),
            P(("dp", "tensor"), None),
        ),
        out_specs=(
            P(("dp", "tensor"), None),
            P(("dp", "tensor"), None),
            P(None, "dp", "tensor"),
            P("tensor", "dp"),
            P("dp", "tensor"),
            P("tensor", "dp"),
            P("dp", None),
            P(None, "dp"),
            P(None, "dp"),
            P("dp"),
        ),
        check_vma=False,
    )
```

profile of v0, /device:TPU:0, one launch (start us, length us, event | category | flops | bytes accessed | tf_op | source)
XLA Modules:
  0.0 1148.0 jit_solution(114364910664673060)
XLA Ops:
  9.5 27.9 %all-gather = bf16[8,96,6]{1,2,0:T(8,128)(2,1)S(1)} all-gather(bf16[1,96,6]{1,2,0:T(8,128)(2,1)S(1)} %convert_bitcast_fusion), channel_id=1, replica_groups=mesh['dp'=8,'tensor'=4] {'dp'}, dimensions={0}, use_global_device_ids=true | all-gather | bytes 10368 | tf_op jit(solution)/shard_map/all_gather | solution.py:151
  39.6 36.3 %all_gather.37 = bf16[3,768,192]{2,0,1:T(4,128)(2,1)S(1)} all-gather(bf16[3,96,192]{2,0,1:T(4,128)(2,1)S(1)} %copy.61), channel_id=1, replica_groups=mesh['dp'=8,'tensor'=4] {'dp'}, dimensions={1}, use_global_device_ids=true | all-gather | bytes 995328 | tf_op jit(solution)/shard_map/all_gather | solution.py:145
  77.0 8.0 scatter_custom_fusion
  85.7 31.1 %all_gather.39 = bf16[192,768]{0,1:T(8,128)(2,1)S(1)} all-gather(bf16[192,96]{0,1:T(8,128)(2,1)S(1)} %copy.66), channel_id=1, replica_groups=mesh['dp'=8,'tensor'=4] {'dp'}, dimensions={1}, use_global_device_ids=true | all-gather | bytes 331776 | tf_op jit(solution)/shard_map/all_gather | solution.py:146
  117.0 12.4 %gather_fusion = bf16[2048,768]{1,0:T(8,128)(2,1)} fusion(bf16[2048,768]{1,0:T(8,128)(2,1)} %all-gather.10.cloned.1.call-done, s32[2048]{0:T(1024)S(1)} %fusion.65), kind=kCustom, calls=%fused_computation | custom fusion | bytes 6299648 | tf_op jit(solution)/shard_map/jit(_take)/gather | solution.py:172
  134.9 49.4 %while.44 = (s32[]{:T(128)}, bf16[4,512,3,64]{1,3,2,0:T(8,128)(2,1)S(1)}, f32[4,3,512]{2,1,0:T(4,128)}, s32[4]{0:T(128)S(1)}, bf16[1,4,512,3,64]{2,4,3,1,0:T(8,1...) while((s32[]{:T(128)}, ...), condition=%wide.region_4.5_spmd.clone, body=%wide.region_1.4_spmd.clone.sunk | while | flops 843055616 | bytes 39975208 | solution.py:62
  140.1 2.8 fusion.135
  142.9 3.7 fusion.136
  155.3 3.7 fusion.136
  167.6 3.7 fusion.136
  179.9 3.7 fusion.136
  189.5 18.1 %all-gather.1 = bf16[8,96,2]{1,2,0:T(2,128)(2,1)S(1)} all-gather(bf16[1,96,2]{1,2,0:T(2,128)(2,1)S(1)} %convert_bitcast_fusion.1), channel_id=1, replica_groups=mesh['dp'=8,'tensor'=4] {'dp'}, dimensions={0}, use_global_device_ids=true | all-gather | bytes 3456 | tf_op jit(solution)/shard_map/all_gather | solution.py:150
  207.7 16.3 %reduce-scatter.20.cloned.1.call-done = bf16[512,768]{1,0:T(8,128)(2,1)} async-done(((bf16[2048,768]{1,0:T(8,128)(2,1)}), bf16[512,768]{1,0:T(8,128)(2,1)}) %reduce-scatter.20.cloned.1.call-update) | async-done | bytes 786448 | tf_op jit(solution)/shard_map/reduce_scatter | solution.py:190
  231.1 26.3 %all-gather.2 = bf16[8,1,384]{2,1,0:T(2,128)(2,1)S(1)} all-gather(bf16[1,1,384]{2,1,0:T(2,128)(2,1)S(1)} %reshape.272), channel_id=1, replica_groups=mesh['dp'=8,'tensor'=4] {'dp'}, dimensions={0}, use_global_device_ids=true | all-gather | bytes 6912 | tf_op jit(solution)/shard_map/all_gather | solution.py:152
  259.3 19.0 %multiply_convert_fusion.1 = (bf16[2048,768]{1,0:T(8,128)(2,1)}, f32[2048,768]{1,0:T(8,128)}, f32[2048,768]{1,0:T(8,128)}) fusion(f32[768]{0:T(1024)S(1)} %dynamic_slice.71, bf16[2048,768]{1,0:T(8,128)(2,1)} %all-gather.12.cloned.1.call-done, bf16[768,768]{1,0:T(8,128)(2,1)} %all-gather.14.cloned.1.call-done), kind=kOutput, calls=%fused_computation.62 | convolution fusion | flops 2519728128 | bytes 20057088 | tf_op jit(solution)/shard_map/dot_general | solution.py:201
  278.3 25.1 %all-gather.16.cloned.1.call-done = bf16[768,768]{0,1:T(8,128)(2,1)} async-done(((bf16[768,96]{0,1:T(8,128)(2,1)}), bf16[768,768]{0,1:T(8,128)(2,1)}) %all-gather.16.cloned.1.call-update) | async-done | bytes 1179664 | tf_op jit(solution)/shard_map/all_gather | solution.py:148
  303.4 6.6 convolution_convert_fusion.1
  311.0 30.6 %all_gather.45 = bf16[768,128]{1,0:T(8,128)(2,1)S(1)} all-gather(bf16[96,128]{1,0:T(8,128)(2,1)S(1)} %convert_element_type.175), channel_id=1, replica_groups=mesh['dp'=8,'tensor'=4] {'dp'}, dimensions={0}, use_global_device_ids=true | all-gather | bytes 221184 | tf_op jit(solution)/shard_map/all_gather | solution.py:149
  341.7 4.5 reduce-scatter.22.cloned.1.call-done
  354.9 28.2 %all-gather.18.cloned.1.call-done = bf16[2048,768]{1,0:T(8,128)(2,1)} async-done(((bf16[512,768]{1,0:T(8,128)(2,1)}), bf16[2048,768]{1,0:T(8,128)(2,1)}) %all-gather.18.cloned.1.call-update) | async-done | bytes 3145744 | tf_op jit(solution)/shard_map/all_gather | solution.py:228
  383.1 11.1 convert_reduce_fusion
  395.9 4.0 convolution_convert_fusion
  400.0 37.8 %reduce-scatter.24.cloned.1.call-done = bf16[512,768]{1,0:T(8,128)(2,1)} async-done(((bf16[2048,768]{1,0:T(8,128)(2,1)}), bf16[512,768]{1,0:T(8,128)(2,1)}) %reduce-scatter.24.cloned.1.call-update) | async-done | bytes 786448 | tf_op jit(solution)/shard_map/reduce_scatter | solution.py:240
  437.8 3.6 multiply_reduce_fusion.2
  444.2 3.0 broadcast.326
  457.9 19.7 %all-gather.20.cloned.1.call-done = bf16[2048,768]{1,0:T(8,128)(2,1)} async-done(((bf16[512,768]{1,0:T(8,128)(2,1)}), bf16[2048,768]{1,0:T(8,128)(2,1)}) %all-gather.20.cloned.1.call-update) | async-done | bytes 3145744 | tf_op jit(solution)/shard_map/all_gather | solution.py:248
  477.6 4.0 convolution_convert_fusion.3
  481.6 3.0 reshape.230
  487.7 119.7 %while.45 = (s32[]{:T(128)}, f32[2048,3,64]{0,2,1:T(8,128)S(1)}, f32[2048,3,64]{0,2,1:T(8,128)}, bf16[4,512,3,64]{1,3,2,0:T(8,128)(2,1)}, s32[4]{0:T(128)S(1)}, ...) while((s32[]{:T(128)}, f32[2048,3,64]{0,2,1:T(8,128)S(1)}, ...), condition=%wide.region_20.21_spmd.clone, body=%wide.region_18.20_spmd.clone.sunk | while | flops 2062516736 | bytes 129419512 | solution.py:113
  494.4 4.9 fusion.148
  499.3 4.8 multiply_reduce_fusion.10
  504.2 5.0 multiply_convert_fusion.3
  509.1 5.7 fusion.149
  523.8 5.5 fusion.148
  529.3 4.8 multiply_reduce_fusion.10
  534.2 5.0 multiply_convert_fusion.3
  539.2 5.6 fusion.149
  553.8 5.5 fusion.148
  559.4 4.8 multiply_reduce_fusion.10
  564.2 5.0 multiply_convert_fusion.3
  569.2 5.6 fusion.149
  583.9 5.5 fusion.148
  589.4 4.8 multiply_reduce_fusion.10
  594.3 5.0 multiply_convert_fusion.3
  599.2 5.6 fusion.149
  613.8 10.6 all-reduce.1
  626.4 4.1 convolution_bitcast_fusion
  630.5 4.6 fusion.58
  635.2 2.9 copy.77
  638.1 4.7 reshape.281
  642.9 13.4 %gather_fusion.2 = f32[2048,768]{1,0:T(8,128)} fusion(f32[2048,768]{1,0:T(8,128)} %get-tuple-element.574, s32[2048]{0:T(1024)S(1)} %broadcast_clamp_fusion), kind=kCustom, calls=%fused_computation.2 | custom fusion | bytes 12591104 | tf_op jit(solution)/shard_map/jit(_take)/gather | solution.py:276
  656.4 7.0 copy.72
  663.3 18.9 %gather_fusion.1 = bf16[2048,3,192]{2,1,0:T(4,128)(2,1)} fusion(bf16[3,2048,192]{2,0,1:T(4,128)(2,1)} %copy.72, s32[2048]{0:T(1024)S(1)} %broadcast_clamp_fusion), kind=kCustom, calls=%fused_computation.1 | custom fusion | bytes 4726784 | tf_op jit(solution)/shard_map/jit(_take)/gather | solution.py:273
  682.2 9.7 select_bitcast_fusion
  691.9 6.2 fusion.48
  700.3 7.0 fusion.81
  707.3 6.9 fusion.82
  716.4 37.2 %all-reduce = f32[3072]{0:T(1024)S(1)} all-reduce(bf16[3072]{0:T(1024)(128)(2,1)S(1)} %get-tuple-element.552), channel_id=13, replica_groups=mesh['dp'=8,'tensor'=4] {'dp'}, use_global_device_ids=true, to_apply=%region_41.42.clone | all-reduce | flops 3072 | bytes 18432
  757.2 62.2 %reduce-scatter.36.cloned.1.call-done = f32[96,192]{1,0:T(8,128)} async-done(((f32[768,192]{1,0:T(8,128)}), f32[96,192]{1,0:T(8,128)}) %reduce-scatter.36.cloned.1.call-update) | async-done | bytes 73744
  821.0 68.1 %reduce-scatter.34.cloned.1.call-done = f32[96,576]{1,0:T(8,128)} async-done(((f32[768,576]{1,0:T(8,128)}), f32[96,576]{1,0:T(8,128)}) %reduce-scatter.34.cloned.1.call-update) | async-done | bytes 221200
  891.0 37.4 %reduce-scatter.26.cloned.1.call-done = bf16[512,768]{1,0:T(8,128)(2,1)} async-done(((bf16[2048,768]{1,0:T(8,128)(2,1)}), bf16[512,768]{1,0:T(8,128)(2,1)}) %reduce-scatter.26.cloned.1.call-update) | async-done | bytes 786448 | tf_op jit(solution)/shard_map/reduce_scatter | solution.py:275
  930.8 63.5 %reduce-scatter.32.cloned.1.call-done = f32[96,128]{1,0:T(8,128)} async-done(((f32[768,128]{1,0:T(8,128)}), f32[96,128]{1,0:T(8,128)}) %reduce-scatter.32.cloned.1.call-update) | async-done | bytes 49168 | tf_op jit(solution)/shard_map/reduce_scatter | solution.py:304
  994.4 73.0 %reduce-scatter.28.cloned.1.call-done = f32[96,768]{1,0:T(8,128)} async-done(((f32[768,768]{1,0:T(8,128)}), f32[96,768]{1,0:T(8,128)}) %reduce-scatter.28.cloned.1.call-update) | async-done | bytes 294928 | tf_op jit(solution)/shard_map/reduce_scatter | solution.py:302
  1067.3 73.1 %reduce-scatter.30.cloned.1.call-done = f32[768,96]{0,1:T(8,128)} async-done(((f32[768,768]{0,1:T(8,128)}), f32[768,96]{0,1:T(8,128)}) %reduce-scatter.30.cloned.1.call-update) | async-done | bytes 294928 | tf_op jit(solution)/shard_map/reduce_scatter | solution.py:303
  (273 shorter events, 125.8 us)
Async XLA Ops:
  8.0 68.9 %copy-start.19 = (s32[1,2048]{1,0:T(1,128)S(1)}, s32[1,2048]{1,0:T(1,128)}, u32[]{:S(2)}) copy-start(s32[1,2048]{1,0:T(1,128)} %param.18) | copy-start | bytes 24580
  8.0 109.0 %all-gather.10.cloned.1.call-start = ((), (), s32[]{:S(2)}) async-start(), calls=%async_computation.11 | async-start | bytes 3932160 | tf_op jit(solution)/shard_map/all_gather | solution.py:166
  8.8 215.3 %reduce-scatter.20.cloned.1.call-start = ((), (), s32[]{:S(2)}) async-start(), calls=%async_computation.12 | async-start | bytes 3932160 | tf_op jit(solution)/shard_map/reduce_scatter | solution.py:190
  76.8 54.7 %copy-start.12 = (bf16[3,768,192]{1,2,0:T(8,128)(2,1)}, bf16[3,768,192]{1,2,0:T(8,128)(2,1)S(1)}, u32[]{:S(2)}) copy-start(bf16[3,768,192]{1,2,0:T(8,128)(2,1)S(1)} %copy.62) | copy-start | bytes 2654212
  76.9 52.4 %copy-start.21 = (s32[2048,1]{0,1:T(1,128)}, s32[2048,1]{0,1:T(1,128)S(1)}, u32[]{:S(2)}) copy-start(s32[2048,1]{0,1:T(1,128)S(1)} %compare_select_fusion) | copy-start | bytes 24580
  131.5 2.1 copy-start.4
  184.3 3.5 copy-start.5
  185.1 2.7 copy-start.7
  185.1 4.4 copy-start.39
  187.8 1.0 copy-start.14
  187.8 69.7 %all-gather.14.cloned.1.call-start = ((), (), s32[]{:S(2)}) async-start(), calls=%async_computation.14 | async-start | bytes 1327104 | tf_op jit(solution)/shard_map/all_gather | solution.py:147
  189.4 69.9 %all-gather.12.cloned.1.call-start = ((), (), s32[]{:S(2)}) async-start(), calls=%async_computation.13 | async-start | bytes 3932160 | tf_op jit(solution)/shard_map/all_gather | solution.py:199
  224.0 3.6 copy-start.1
  224.0 6.2 copy-start.15
  224.0 7.0 copy-start.37
  227.7 3.4 copy-start.26
  230.2 73.2 %all-gather.16.cloned.1.call-start = ((), (), s32[]{:S(2)}) async-start(), calls=%async_computation.15 | async-start | bytes 1327104 | tf_op jit(solution)/shard_map/all_gather | solution.py:148
  231.0 115.2 %reduce-scatter.22.cloned.1.call-start = ((), (), s32[]{:S(2)}) async-start(), calls=%async_computation.16 | async-start | bytes 3932160 | tf_op jit(solution)/shard_map/reduce_scatter | solution.py:203
  257.5 20.9 %copy-start.35 = (f32[768]{0:T(1024)}, f32[768]{0:T(1024)S(1)}, u32[]{:S(2)}) copy-start(f32[768]{0:T(1024)S(1)} %dynamic_slice.71) | copy-start | bytes 9220
  310.0 0.8 copy-start.17
  310.0 0.9 copy-start.16
  310.0 36.2 %copy-start.18 = (f32[768]{0:T(1024)S(1)}, f32[768]{0:T(1024)}, u32[]{:S(2)}) copy-start(f32[768]{0:T(1024)} %get-tuple-element.508) | copy-start | bytes 9220
  310.0 36.2 %copy-start.28 = (f32[768]{0:T(1024)S(1)}, f32[768]{0:T(1024)}, u32[]{:S(2)}) copy-start(f32[768]{0:T(1024)} %get-tuple-element.507) | copy-start | bytes 9220
  310.0 38.7 %copy-start.27 = (f32[768]{0:T(1024)S(1)}, f32[768]{0:T(1024)}, u32[]{:S(2)}) copy-start(f32[768]{0:T(1024)} %get-tuple-element.506) | copy-start | bytes 9220
  310.0 73.1 %all-gather.18.cloned.1.call-start = ((), (), s32[]{:S(2)}) async-start(), calls=%async_computation.17 | async-start | bytes 3932160 | tf_op jit(solution)/shard_map/all_gather | solution.py:228
  349.0 2.5 copy-start.6
  350.2 2.0 copy-start.10
  351.6 31.6 %copy-start.36 = (f32[768]{0:T(1024)S(1)}, f32[768]{0:T(1024)}, u32[]{:S(2)}) copy-start(f32[768]{0:T(1024)} %copy-done.35) | copy-start | bytes 9220
  352.2 1.1 copy-start.2
  352.2 42.0 %copy-start.23 = (f32[512]{0:T(512)}, f32[512]{0:T(512)S(1)}, u32[]{:S(2)}) copy-start(f32[512]{0:T(512)S(1)} %negate_multiply_fusion.2) | copy-start | bytes 6148
  354.5 83.3 %reduce-scatter.24.cloned.1.call-start = ((), (), s32[]{:S(2)}) async-start(), calls=%async_computation.18 | async-start | bytes 3932160 | tf_op jit(solution)/shard_map/reduce_scatter | solution.py:240
  383.1 12.8 %copy-start.38 = (bf16[768,768]{1,0:T(8,128)(2,1)S(1)}, bf16[768,768]{1,0:T(8,128)(2,1)}, u32[]{:S(2)}) copy-start(bf16[768,768]{1,0:T(8,128)(2,1)} %all-gather.14.cloned.1.call-done) | copy-start | bytes 3538948
  394.3 1.6 copy-start.41
  399.9 77.7 %all-gather.20.cloned.1.call-start = ((), (), s32[]{:S(2)}) async-start(), calls=%async_computation.19 | async-start | bytes 3932160 | tf_op jit(solution)/shard_map/all_gather | solution.py:248
  437.8 4.3 copy-start.3
  437.8 4.3 copy-start.9
  447.2 2.4 copy-start.34
  448.9 249.3 %all-reduce.4.cloned.1.call-start = ((), (), s32[]{:S(2)}) async-start(), calls=%async_computation.23 | async-start | bytes 393216 | tf_op jit(solution)/shard_map/psum | solution.py:294
  452.5 301.7 %reduce-scatter.38.cloned.1.call-start = ((), (), s32[]{:S(2)}) async-start(), calls=%async_computation.27 | async-start | bytes 442368
  453.6 33.1 %copy-start.24 = (bf16[3072]{0:T(1024)(128)(2,1)}, bf16[3072]{0:T(1024)(128)(2,1)S(1)}, u32[]{:S(2)}) copy-start(bf16[3072]{0:T(1024)(128)(2,1)S(1)} %dynamic_update_slice.46) | copy-start | bytes 18436
  509.1 5.7 copy-start
  539.2 5.6 copy-start
  569.2 5.6 copy-start
  599.2 5.6 copy-start
  609.9 3.8 copy-start.30
  609.9 3.8 copy-start.31
  609.9 3.8 copy-start.32
  609.9 3.8 copy-start.33
  609.9 3.8 copy-start.25
  609.9 3.8 copy-start.29
  611.4 14.9 %copy-start.8 = (bf16[24,8,4,512]{3,1,2,0:T(8,128)(2,1)S(1)}, bf16[24,8,4,512]{3,1,2,0:T(8,128)(2,1)}, u32[]{:S(2)}) copy-start(bf16[24,8,4,512]{3,1,2,0:T(8,128)(2,1)} %copy-done.7) | copy-start | bytes 2359300
  625.3 130.4 %reduce-scatter.40.cloned.1.call-start = ((), (), s32[]{:S(2)}) async-start(), calls=%async_computation.28 | async-start | bytes 442368
  626.3 193.1 %reduce-scatter.36.cloned.1.call-start = ((), (), s32[]{:S(2)}) async-start(), calls=%async_computation.26 | async-start | bytes 884736
  630.5 258.6 %reduce-scatter.34.cloned.1.call-start = ((), (), s32[]{:S(2)}) async-start(), calls=%async_computation.25 | async-start | bytes 2211840
  638.1 4.8 copy-start.20
  638.1 4.8 copy-start.22
  642.8 285.6 %reduce-scatter.26.cloned.1.call-start = ((), (), s32[]{:S(2)}) async-start(), calls=%async_computation.20 | async-start | bytes 3932160 | tf_op jit(solution)/shard_map/reduce_scatter | solution.py:275
  682.2 9.7 copy-start.13
  698.2 296.2 %reduce-scatter.32.cloned.1.call-start = ((), (), s32[]{:S(2)}) async-start(), calls=%async_computation.24 | async-start | bytes 442368 | tf_op jit(solution)/shard_map/reduce_scatter | solution.py:304
  700.0 367.3 %reduce-scatter.28.cloned.1.call-start = ((), (), s32[]{:S(2)}) async-start(), calls=%async_computation.21 | async-start | bytes 2654208 | tf_op jit(solution)/shard_map/reduce_scatter | solution.py:302
  707.3 7.1 copy-start.40
  707.3 8.3 copy-start.11
  707.3 433.1 %reduce-scatter.30.cloned.1.call-start = ((), (), s32[]{:S(2)}) async-start(), calls=%async_computation.22 | async-start | bytes 2654208 | tf_op jit(solution)/shard_map/reduce_scatter | solution.py:303
Sparse Core Ops, SparseCore 0:
  10.4 31.2 all-gather.9
  187.9 36.0 reduce-scatter.19
  354.6 28.5 all-gather.17
  449.0 28.4 all-gather.19
  480.3 31.9 all-reduce.3
Sparse Core Ops, SparseCore 1:
  191.0 39.5 all-gather.13
  232.6 26.7 all-gather.11
  262.0 41.4 all-gather.15
  310.1 36.0 reduce-scatter.21
  400.0 37.7 reduce-scatter.23
  625.4 63.2 reduce-scatter.37
  691.8 61.3 reduce-scatter.39
  756.9 62.4 reduce-scatter.35
  822.7 66.3 reduce-scatter.33
  891.7 36.7 reduce-scatter.25
  932.2 62.2 reduce-scatter.31
  998.5 68.8 reduce-scatter.27
  1071.3 69.1 reduce-scatter.29
where the time goes:
time: 1150 us
  waiting for transfers between devices  512 us (45%)
  blocking collectives  218 us (19%)
  matrix products  189 us (16%)
  local copies, waits for them, and re-layouts  112 us (10%)
  other arithmetic  81.9 us (7%)
  between operations  18 us (2%)
  loops' own time  16 us (1%)
    unnamed x22, waiting for transfers between devices  131 us
    reduce_scatter x1, waiting for transfers between devices, body(): lax.psum_scatter(grad_down, 'dp', scatter_dimension=1, tiled=True)  73.1 us
    reduce_scatter x1, waiting for transfers between devices, body(): lax.psum_scatter(grad_up, 'dp', scatter_dimension=0, tiled=True)  73 us
    reduce_scatter x1, waiting for transfers between devices, body(): lax.psum_scatter(grad_proj, 'dp', scatter_dimension=0, tiled=True)  63.5 us
    reduce_scatter x1, waiting for transfers between devices, body(): lax.psum_scatter(times_transposed(dpre_low, up_weight).astype(jnp.bfloat1...  37.8 us
    reduce_scatter x1, waiting for transfers between devices, body(): lax.psum_scatter((through + jnp.take(resid_full, slot_order, axis=0)).ast...  37.4 us
    unnamed x1, blocking collectives  37.2 us
    all_gather x1, blocking collectives, body(): lax.all_gather(w_qkv.astype(jnp.bfloat16), 'dp', axis=1, tiled=True)  36.3 us
  transfers between devices with their start and end apart: 18, of which 13 were waited for; matrix products, arithmetic and copies ran while one was open for 24% of the time, Pallas kernels for 0%

commit v1 on v0

--- a/solution.py
+++ b/solution.py
@@ -1,6 +1,10 @@
+import functools
+
 import jax
 import jax.numpy as jnp
 from jax import lax
+from jax.experimental import pallas as pl
+from jax.experimental.pallas import tpu as pltpu
 from jax.sharding import PartitionSpec as P
 
 HEAD_DIM = 64
@@ -118,6 +122,476 @@
     return lax.map(passage, jnp.arange(key_heads.shape[0]))
 
 
+MESH = pl.DeviceIdType.MESH
+VMEM = pl.BlockSpec(memory_space=pltpu.VMEM)
+RING_MAX = 8
+ROW_PIECES = 4
+
+
+def ring_place(position, size):
+    far = position // (size // 2)
+    return 2 * ((1 - far) * position + far * (size - 1 - position)) + far
+
+
+def ring_position(index, size):
+    row, far = index // 2, index % 2
+    return (1 - far) * row + far * (size - 1 - row)
+
+
+def ring_hops(index, size):
+    longer, shorter = size // 2, size - 1 - size // 2
+    return (longer, shorter) if index % 2 == 0 else (shorter, longer)
+
+
+class Ring:
+    def __init__(self, size):
+        self.size = size
+        self.me = lax.axis_index("dp")
+        self.position = ring_position(self.me, size)
+        self.targets = (self.at(1), self.at(-1))
+
+    def at(self, offset):
+        return ring_place(lax.rem(self.position + (offset + self.size), self.size), self.size)
+
+
+class Chip:
+    def __init__(self):
+        self.me = lax.axis_index("tensor")
+        chip, core = self.me // 2, self.me % 2
+        self.mate = 2 * chip + (1 - core)
+        self.peer = 2 * (1 - chip) + core
+        self.across = 2 * (1 - chip) + (1 - core)
+
+
+def greet(devices):
+    barrier = pltpu.get_barrier_semaphore()
+    for device in devices:
+        pl.semaphore_signal(barrier, inc=1, device_id=device, device_id_type=MESH)
+    pl.semaphore_wait(barrier, len(devices))
+
+
+def remote(source, target, send, recv, device):
+    return pltpu.make_async_remote_copy(
+        src_ref=source,
+        dst_ref=target,
+        send_sem=send,
+        recv_sem=recv,
+        device_id=device,
+        device_id_type=MESH,
+    )
+
+
+class RingGather:
+    def __init__(self, ring, shards, outs, send, recv):
+        self.ring, self.shards, self.outs, self.send, self.recv = ring, shards, outs, send, recv
+
+    def copy(self, i, way, hop):
+        owner = self.ring.at(-hop if way == 0 else hop)
+        target = self.outs[i].at[owner]
+        return remote(
+            self.shards[i] if hop == 0 else target,
+            target,
+            self.send.at[i, way, hop],
+            self.recv.at[i, way, hop],
+            {"dp": self.ring.targets[way]},
+        )
+
+    def each(self, hop):
+        for i in range(len(self.shards)):
+            for way in (0, 1):
+                if hop < ring_hops(i, self.ring.size)[way]:
+                    yield i, way
+
+    def start(self):
+        for i, way in self.each(0):
+            self.copy(i, way, 0).start()
+        for shard, out in zip(self.shards, self.outs):
+            out[self.ring.me] = shard[...]
+
+    def relay(self, hop):
+        for i, way in self.each(hop - 1):
+            self.copy(i, way, hop - 1).wait_recv()
+            if hop < ring_hops(i, self.ring.size)[way]:
+                self.copy(i, way, hop).start()
+
+    def finish(self):
+        for hop in range(self.ring.size // 2):
+            for i, way in self.each(hop):
+                self.copy(i, way, hop).wait_send()
+
+
+class RingScatter:
+    def __init__(self, ring, parts, landing, send, recv):
+        self.ring, self.parts, self.landing, self.send, self.recv = ring, parts, landing, send, recv
+
+    def slot(self, i, way, hop):
+        return self.landing[i].at[hop + (0 if way == 0 else ring_hops(i, self.ring.size)[0])]
+
+    def owner(self, i, way, hop):
+        left = ring_hops(i, self.ring.size)[way] - hop
+        return self.ring.at(left if way == 0 else -left)
+
+    def copy(self, i, way, hop):
+        source = self.parts[i].at[self.owner(i, way, 0)] if hop == 0 else self.slot(i, way, hop - 1)
+        return remote(
+            source,
+            self.slot(i, way, hop),
+            self.send.at[i, way, hop],
+            self.recv.at[i, way, hop],
+            {"dp": self.ring.targets[way]},
+        )
+
+    def each(self, hop):
+        for i in range(len(self.parts)):
+            for way in (0, 1):
+                if hop < ring_hops(i, self.ring.size)[way]:
+                    yield i, way
+
+    def start(self):
+        for i, way in self.each(0):
+            self.copy(i, way, 0).start()
+
+    def relay(self, hop):
+        for i, way in self.each(hop - 1):
+            self.copy(i, way, hop - 1).wait_recv()
+            if hop < ring_hops(i, self.ring.size)[way]:
+                slot = self.slot(i, way, hop - 1)
+                own = self.parts[i][self.owner(i, way, hop)]
+                slot[...] = (slot[...].astype(jnp.float32) + own.astype(jnp.float32)).astype(slot.dtype)
+                self.copy(i, way, hop).start()
+
+    def total(self, i):
+        up, down = ring_hops(i, self.ring.size)
+        return (
+            self.parts[i][self.ring.me].astype(jnp.float32)
+            + self.slot(i, 0, up - 1)[...].astype(jnp.float32)
+            + self.slot(i, 1, down - 1)[...].astype(jnp.float32)
+        )
+
+    def finish(self):
+        for hop in range(self.ring.size // 2):
+            for i, way in self.each(hop):
+                self.copy(i, way, hop).wait_send()
+
+
+class RowGather:
+    def __init__(self, chip, own, out, send, recv):
+        self.chip, self.own, self.out, self.send, self.recv = chip, own, out, send, recv
+        self.step = own.shape[0] // ROW_PIECES
+
+    def copy(self, kind, piece):
+        rows = pl.ds(piece * self.step, self.step)
+        chip = self.chip
+        owner = chip.peer if kind == 2 else chip.me
+        target = self.out.at[owner, rows]
+        device = chip.peer if kind == 0 else chip.mate
+        return remote(
+            target if kind == 2 else self.own.at[rows],
+            target,
+            self.send.at[kind, piece],
+            self.recv.at[kind, piece],
+            {"tensor": device},
+        )
+
+    def start(self):
+        for kind in (0, 1):
+            for piece in range(ROW_PIECES):
+                self.copy(kind, piece).start()
+        self.out[self.chip.me] = self.own[...]
+
+    def relay(self, piece):
+        self.copy(0, piece).wait_recv()
+        self.copy(2, piece).start()
+
+    def finish(self):
+        for kind in (1, 2):
+            for piece in range(ROW_PIECES):
+                self.copy(kind, piece).wait_recv()
+        for kind in (0, 1, 2):
+            for piece in range(ROW_PIECES):
+                self.copy(kind, piece).wait_send()
+
+
+class RowScatter:
+    def __init__(self, chip, parts, landing, send, recv):
+        self.chip, self.parts, self.landing, self.send, self.recv = chip, parts, landing, send, recv
+        self.step = parts.shape[1] // ROW_PIECES
+
+    def rows(self, piece):
+        return pl.ds(piece * self.step, self.step)
+
+    def copy(self, kind, piece):
+        chip, rows = self.chip, self.rows(piece)
+        source = (
+            self.parts.at[chip.across, rows],
+            self.landing.at[0, rows],
+            self.parts.at[chip.mate, rows],
+        )[kind]
+        return remote(
+            source,
+            self.landing.at[kind, rows],
+            self.send.at[kind, piece],
+            self.recv.at[kind, piece],
+            {"tensor": chip.peer if kind == 1 else chip.mate},
+        )
+
+    def start(self):
+        for kind in (0, 2):
+            for piece in range(ROW_PIECES):
+                self.copy(kind, piece).start()
+
+    def relay(self, piece):
+        rows = self.rows(piece)
+        self.copy(0, piece).wait_recv()
+        total = self.landing[0, rows].astype(jnp.float32) + self.parts[self.chip.peer, rows].astype(
+            jnp.float32
+        )
+        self.landing[0, rows] = total.astype(self.landing.dtype)
+        self.copy(1, piece).start()
+
+    def total(self, piece):
+        rows = self.rows(piece)
+        self.copy(2, piece).wait_recv()
+        self.copy(1, piece).wait_recv()
+        return (
+            self.parts[self.chip.me, rows].astype(jnp.float32)
+            + self.landing[1, rows].astype(jnp.float32)
+            + self.landing[2, rows].astype(jnp.float32)
+        )
+
+    def finish(self):
+        for kind in (0, 1, 2):
+            for piece in range(ROW_PIECES):
+                self.copy(kind, piece).wait_send()
+
+
+def row_sems():
+    return [pltpu.SemaphoreType.DMA((3, ROW_PIECES))] * 2
+
+
+def ring_sems(count, size):
+    return [pltpu.SemaphoreType.DMA((count, 2, size // 2))] * 2
+
+
+def comm_params(collective_id):
+    return pltpu.CompilerParams(collective_id=collective_id, has_side_effects=True)
+
+
+def gather_rows(own, collective_id):
+    def kernel(own_ref, out_ref, send, recv):
+        chip = Chip()
+        greet(({"tensor": chip.mate}, {"tensor": chip.peer}))
+        rows = RowGather(chip, own_ref, out_ref, send, recv)
+        rows.start()
+        for piece in range(ROW_PIECES):
+            rows.relay(piece)
+        rows.finish()
+
+    out = pl.pallas_call(
+        kernel,
+        out_shape=jax.ShapeDtypeStruct((4, *own.shape), own.dtype),
+        in_specs=[VMEM],
+        out_specs=VMEM,
+        scratch_shapes=row_sems(),
+        compiler_params=comm_params(collective_id),
+        name="gather_rows",
+    )(own)
+    return out.reshape(4 * own.shape[0], own.shape[1])
+
+
+def scatter_rows(parts, collective_id):
+    parts = parts.reshape(4, parts.shape[0] // 4, parts.shape[1])
+
+    def kernel(parts_ref, out_ref, landing, send, recv):
+        chip = Chip()
+        greet(({"tensor": chip.mate}, {"tensor": chip.peer}))
+        rows = RowScatter(chip, parts_ref, landing, send, recv)
+        rows.start()
+        for piece in range(ROW_PIECES):
+            rows.relay(piece)
+        for piece in range(ROW_PIECES):
+            out_ref[rows.rows(piece)] = rows.total(piece)
+        rows.finish()
+
+    return pl.pallas_call(
+        kernel,
+        out_shape=jax.ShapeDtypeStruct(parts.shape[1:], jnp.float32),
+        in_specs=[VMEM],
+        out_specs=VMEM,
+        scratch_shapes=[pltpu.VMEM((3, *parts.shape[1:]), parts.dtype)] + row_sems(),
+        compiler_params=comm_params(collective_id),
+        name="scatter_rows",
+    )(parts)
+
+
+def gather_all(shards, own, size, collective_id):
+    if size > RING_MAX:
+        return [lax.all_gather(shard, "dp") for shard in shards], gather_rows(own, collective_id)
+    count = len(shards)
+
+    def kernel(*refs):
+        shard_refs, own_ref = refs[:count], refs[count]
+        out_refs, rows_ref = refs[count + 1 : 2 * count + 1], refs[2 * count + 1]
+        ring_send, ring_recv, row_send, row_recv = refs[2 * count + 2 :]
+        ring, chip = Ring(size), Chip()
+        greet(
+            (
+                {"dp": ring.targets[0]},
+                {"dp": ring.targets[1]},
+                {"tensor": chip.mate},
+                {"tensor": chip.peer},
+            )
+        )
+        rows = RowGather(chip, own_ref, rows_ref, row_send, row_recv)
+        weights = RingGather(ring, shard_refs, out_refs, ring_send, ring_recv)
+        rows.start()
+        weights.start()
+        for hop in range(1, size // 2 + 1):
+            for piece in range(ROW_PIECES):
+                if piece * (size // 2) // ROW_PIECES == hop - 1:
+                    rows.relay(piece)
+            weights.relay(hop)
+        rows.finish()
+        weights.finish()
+
+    *gathered, arrived = pl.pallas_call(
+        kernel,
+        out_shape=[jax.ShapeDtypeStruct((size, *s.shape), s.dtype) for s in shards]
+        + [jax.ShapeDtypeStruct((4, *own.shape), own.dtype)],
+        in_specs=[VMEM] * (count + 1),
+        out_specs=[VMEM] * (count + 1),
+        scratch_shapes=ring_sems(count, size) + row_sems(),
+        compiler_params=comm_params(collective_id),
+        name="gather_all",
+    )(*shards, own)
+    return gathered, arrived.reshape(4 * own.shape[0], own.shape[1])
+
+
+def scatter_all(parts, shared, rows_part, size, collective_id):
+    if size > RING_MAX:
+        summed = [lax.psum_scatter(p.astype(jnp.float32), "dp", scatter_dimension=0) for p in parts]
+        summed[-shared:] = [lax.psum(s, "tensor") for s in summed[-shared:]]
+        return summed, scatter_rows(rows_part, collective_id)
+    count = len(parts)
+    rows_part = rows_part.reshape(4, rows_part.shape[0] // 4, rows_part.shape[1])
+
+    def kernel(*refs):
+        part_refs, rows_ref = refs[:count], refs[count]
+        out_refs, own_ref = refs[count + 1 : 2 * count + 1], refs[2 * count + 1]
+        scratch = refs[2 * count + 2 :]
+        landing, row_landing = scratch[:count], scratch[count]
+        meets = scratch[count + 1 : count + 1 + shared]
+        ring_send, ring_recv, row_send, row_recv, meet_send, meet_recv = scratch[count + 1 + shared :]
+        ring, chip = Ring(size), Chip()
+        others = (chip.mate, chip.peer, chip.across)
+        greet(
+            ({"dp": ring.targets[0]}, {"dp": ring.targets[1]})
+            + tuple({"tensor": other} for other in others)
+        )
+        rows = RowScatter(chip, rows_ref, row_landing, row_send, row_recv)
+        grads = RingScatter(ring, part_refs, landing, ring_send, ring_recv)
+        rows.start()
+        grads.start()
+        for hop in range(1, size // 2 + 1):
+            for piece in range(ROW_PIECES):
+                if piece * (size // 2) // ROW_PIECES == hop - 1:
+                    rows.relay(piece)
+            grads.relay(hop)
+        copies = []
+        for j in range(shared):
+            meets[j][chip.me] = grads.total(count - shared + j)
+            for k, other in enumerate(others):
+                copy = remote(
+                    meets[j].at[chip.me],
+                    meets[j].at[chip.me],
+                    meet_send.at[j, k],
+                    meet_recv.at[j, k],
+                    {"tensor": other},
+                )
+                copy.start()
+                copies.append(copy)
+        for i in range(count - shared):
+            out_refs[i][...] = grads.total(i)
+        for piece in range(ROW_PIECES):
+            own_ref[rows.rows(piece)] = rows.total(piece)
+        for copy in copies:
+            copy.wait_recv()
+        for j in range(shared):
+            out_refs[count - shared + j][...] = (meets[j][0] + meets[j][1]) + (meets[j][2] + meets[j][3])
+        rows.finish()
+        grads.finish()
+        for copy in copies:
+            copy.wait_send()
+
+    f32 = jnp.float32
+    *summed, own = pl.pallas_call(
+        kernel,
+        out_shape=[jax.ShapeDtypeStruct(p.shape[1:], f32) for p in parts]
+        + [jax.ShapeDtypeStruct(rows_part.shape[1:], f32)],
+        in_specs=[VMEM] * (count + 1),
+        out_specs=[VMEM] * (count + 1),
+        scratch_shapes=[pltpu.VMEM((size - 1, *p.shape[1:]), p.dtype) for p in parts]
+        + [pltpu.VMEM((3, *rows_part.shape[1:]), rows_part.dtype)]
+        + [pltpu.VMEM((4, *p.shape[1:]), f32) for p in parts[-shared:]]
+        + ring_sems(count, size)
+        + row_sems()
+        + [pltpu.SemaphoreType.DMA((shared, 3))] * 2,
+        compiler_params=comm_params(collective_id),
+        name="scatter_all",
+    )(*parts, rows_part)
+    return summed, own
+
+
+def enter_slots(slots, arrived, weight, shift):
+    group, width = arrived.shape
+    block = 256
+
+    def kernel(slots_ref, arrived_ref, weight_ref, shift_ref, rows_ref, out_ref):
+        first = pl.program_id(0) * block
+        wanted = first + lax.broadcasted_iota(jnp.int32, (block, group), 0)
+        pick = jnp.where(slots_ref[...] == wanted, 1.0, 0.0).astype(jnp.bfloat16)
+        rows = jnp.dot(pick, arrived_ref[...], preferred_element_type=jnp.float32).astype(jnp.bfloat16)
+        rows_ref[...] = rows
+        out = jnp.dot(rows, weight_ref[...], preferred_element_type=jnp.float32) + shift_ref[...]
+        out_ref[...] = out.astype(jnp.bfloat16)
+
+    return pl.pallas_call(
+        kernel,
+        grid=(group // block,),
+        in_specs=[VMEM] * 4,
+        out_specs=[
+            pl.BlockSpec((block, width), lambda i: (i, 0)),
+            pl.BlockSpec((block, weight.shape[1]), lambda i: (i, 0)),
+        ],
+        out_shape=[
+            jax.ShapeDtypeStruct((group, width), jnp.bfloat16),
+            jax.ShapeDtypeStruct((group, weight.shape[1]), jnp.bfloat16),
+        ],
+        name="enter_slots",
+    )(slots.reshape(1, group), arrived, weight, shift.reshape(1, -1))
+
+
+def leave_slots(slots, rows):
+    group, width = rows.shape
+    block = 256
+
+    def kernel(slots_ref, rows_ref, out_ref):
+        slot = lax.broadcasted_iota(jnp.int32, (block, group), 1)
+        pick = jnp.where(slots_ref[...] == slot, 1.0, 0.0).astype(jnp.bfloat16)
+        out_ref[...] = jnp.dot(pick, rows_ref[...], preferred_element_type=jnp.float32).astype(
+            jnp.bfloat16
+        )
+
+    return pl.pallas_call(
+        kernel,
+        grid=(group // block,),
+        in_specs=[pl.BlockSpec((block, 1), lambda i: (i, 0)), VMEM],
+        out_specs=pl.BlockSpec((block, width), lambda i: (i, 0)),
+        out_shape=jax.ShapeDtypeStruct((group, width), jnp.bfloat16),
+        name="leave_slots",
+    )(slots.reshape(group, 1), rows)
+
+
 def body(
     tokens,
     lengths,
@@ -141,71 +615,56 @@
     num_blocks = SLOT // block_rows
     factor = HEAD_DIM ** (-0.5)
     slot_order = arrival_slots[0]
-    gathered = (
-        lax.all_gather(w_qkv.astype(jnp.bfloat16), "dp", axis=1, tiled=True),
-        lax.all_gather(w_out.astype(jnp.bfloat16), "dp", axis=1, tiled=True),
-        lax.all_gather(w_up.astype(jnp.bfloat16), "dp", axis=0, tiled=True),
-        lax.all_gather(w_down.astype(jnp.bfloat16), "dp", axis=1, tiled=True),
-        lax.all_gather(w_proj.astype(jnp.bfloat16), "dp", axis=0, tiled=True),
-        lax.all_gather(norm_gains.astype(jnp.bfloat16), "dp", axis=1, tiled=True),
-        lax.all_gather(biases.astype(jnp.bfloat16), "dp", axis=1, tiled=True),
-        lax.all_gather(up_bias.astype(jnp.bfloat16), "dp", axis=0, tiled=True),
-    )
-    qkv_weight, out_weight, up_weight, down_weight, proj_weight, gain_low, bias_low, upbias_low = (
-        gathered
-    )
-    width_local = qkv_weight.shape[2]
+    size = lax.axis_size("dp")
+    part_rows, width_local = w_qkv.shape[1:]
+    low = jnp.bfloat16
+    shards = [
+        w_qkv.astype(low).transpose(1, 0, 2).reshape(part_rows, 3 * width_local),
+        w_up.astype(low),
+        w_out.astype(low).T,
+        w_down.astype(low).T,
+        w_proj.astype(low),
+        jnp.concatenate(
+            [norm_gains.astype(low), biases.astype(low), up_bias.astype(low).reshape(-1, part_rows)]
+        ),
+    ]
+    gathered, arrived = gather_all(shards, tokens, size, 0)
+    width = size * part_rows
+    qkv_weight, up_weight, out_weight, down_weight, proj_weight = (
+        g.reshape(width, g.shape[2]) for g in gathered[:5]
+    )
+    small = gathered[5].astype(jnp.float32)
+    side = small[:, :8].transpose(1, 0, 2).reshape(8, width)
+    gain_full, bias_full = side[:2], side[2:]
+    upbias_full = small[:, 8:].reshape(-1)
     hidden_local = up_weight.shape[1]
     heads_local = width_local // HEAD_DIM
-    gain_full = gain_low.astype(jnp.float32)
-    bias_full = bias_low.astype(jnp.float32)
-    upbias_full = upbias_low.astype(jnp.float32)
     col_start = tensor_pos * width_local
     query_bias = lax.dynamic_slice_in_dim(bias_full[0], col_start, width_local)
     value_bias = lax.dynamic_slice_in_dim(bias_full[1], col_start, width_local)
-    arrived = lax.all_gather(tokens, "tensor", axis=0, tiled=True)
-    inverse = (
-        jnp.zeros((group_rows,), jnp.int32)
-        .at[slot_order]
-        .set(jnp.arange(group_rows, dtype=jnp.int32))
-    )
-    slotted = jnp.take(arrived, inverse, axis=0)
+    qkv_bias = jnp.concatenate([query_bias, jnp.zeros_like(query_bias), value_bias])
+    slotted, qkv_all = enter_slots(slot_order, arrived, qkv_weight, qkv_bias)
     row_start = tensor_pos * own_rows
     resid_input = lax.dynamic_slice_in_dim(slotted, row_start, own_rows, 0).astype(jnp.float32)
     positions = row_start + jnp.arange(own_rows, dtype=jnp.int32)
     row_keep = (positions % SLOT < lengths[positions // SLOT]).astype(jnp.float32)
     key_mask = jnp.arange(SLOT, dtype=jnp.int32)[None, :] < lengths[:, None]
-    qkv_bias = jnp.stack([query_bias, jnp.zeros_like(query_bias), value_bias])
-    qkv_all = (
-        jnp.einsum("gd,cde->cge", slotted, qkv_weight, preferred_element_type=jnp.float32)
-        + qkv_bias[:, None, :]
-    ).astype(jnp.bfloat16)
     block_shape = (passages, num_blocks, block_rows, heads_local, HEAD_DIM)
     slot_shape = (passages, SLOT, heads_local, HEAD_DIM)
-    query_heads = qkv_all[0].reshape(block_shape)
-    key_heads = qkv_all[1].reshape(slot_shape)
-    value_heads = qkv_all[2].reshape(slot_shape)
+    query_heads = qkv_all[:, 0 * width_local : 1 * width_local].reshape(block_shape)
+    key_heads = qkv_all[:, 1 * width_local : 2 * width_local].reshape(slot_shape)
+    value_heads = qkv_all[:, 2 * width_local : 3 * width_local].reshape(slot_shape)
     attended, log_total = attend(query_heads, key_heads, value_heads, key_mask, num_blocks, factor)
     context = attended.reshape(group_rows, width_local).astype(jnp.bfloat16)
-    attn_part = lax.psum_scatter(
-        jnp.dot(context, out_weight, preferred_element_type=jnp.float32).astype(jnp.bfloat16),
-        "tensor",
-        scatter_dimension=0,
-        tiled=True,
-    ).astype(jnp.float32)
+    attn_part = scatter_rows(times_transposed(context, out_weight).astype(low), 1)
     first_sum = resid_input + attn_part + bias_full[2]
     first_norm, back_first = jax.vjp(norm_rows, first_sum, gain_full[0], bias_full[3])
     first_low = first_norm.astype(jnp.bfloat16)
-    mid_rows = lax.all_gather(first_low, "tensor", axis=0, tiled=True)
+    mid_rows = gather_rows(first_low, 2)
     upbias_own = lax.dynamic_slice_in_dim(upbias_full, tensor_pos * hidden_local, hidden_local)
     ffn_pre = jnp.dot(mid_rows, up_weight, preferred_element_type=jnp.float32) + upbias_own
     hidden = gelu_exact(ffn_pre).astype(jnp.bfloat16)
-    ffn_part = lax.psum_scatter(
-        jnp.dot(hidden, down_weight, preferred_element_type=jnp.float32).astype(jnp.bfloat16),
-        "tensor",
-        scatter_dimension=0,
-        tiled=True,
-    ).astype(jnp.float32)
+    ffn_part = scatter_rows(times_transposed(hidden, down_weight).astype(low), 3)
     second_sum = first_norm + ffn_part + bias_full[4]
     second_norm, back_second = jax.vjp(norm_rows, second_sum, gain_full[1], bias_full[5])
     second_low = second_norm.astype(jnp.bfloat16)
@@ -225,9 +684,9 @@
     dsecond_norm = times_transposed(dproj_low, proj_weight)
     dsecond, grad_gain_two, grad_shift_two = back_second(dsecond_norm)
     dsecond_low = dsecond.astype(jnp.bfloat16)
-    dsecond_rows = lax.all_gather(dsecond_low, "tensor", axis=0, tiled=True)
-    dhidden = times_transposed(dsecond_rows, down_weight)
-    grad_down = contract_rows(hidden, dsecond_rows)
+    dsecond_rows = gather_rows(dsecond_low, 4)
+    dhidden = jnp.dot(dsecond_rows, down_weight, preferred_element_type=jnp.float32)
+    grad_down = contract_rows(dsecond_rows, hidden)
     (dpre,) = jax.vjp(gelu_exact, ffn_pre)[1](dhidden)
     dpre_low = dpre.astype(jnp.bfloat16)
     grad_upbias = lax.dynamic_update_slice_in_dim(
@@ -237,17 +696,12 @@
         0,
     )
     grad_up = contract_rows(mid_rows, dpre_low)
-    dfirst_norm = lax.psum_scatter(
-        times_transposed(dpre_low, up_weight).astype(jnp.bfloat16),
-        "tensor",
-        scatter_dimension=0,
-        tiled=True,
-    ).astype(jnp.float32)
+    dfirst_norm = scatter_rows(times_transposed(dpre_low, up_weight).astype(low), 5)
     dfirst, grad_gain_one, grad_shift_one = back_first(dfirst_norm + dsecond)
     dfirst_low = dfirst.astype(jnp.bfloat16)
-    dfirst_rows = lax.all_gather(dfirst_low, "tensor", axis=0, tiled=True)
-    dcontext = times_transposed(dfirst_rows, out_weight).astype(jnp.bfloat16)
-    grad_out = contract_rows(context, dfirst_rows)
+    dfirst_rows = gather_rows(dfirst_low, 6)
+    dcontext = jnp.dot(dfirst_rows, out_weight, preferred_element_type=jnp.float32).astype(low)
+    grad_out = contract_rows(dfirst_rows, context)
     dquery, dkey, dvalue = attend_back(
         query_heads,
         key_heads,
@@ -258,26 +712,20 @@
         num_blocks,
         factor,
     )
-    dqkv = jnp.stack(
+    dqkv = jnp.concatenate(
         [
             dquery.reshape(group_rows, width_local),
             dkey.reshape(group_rows, width_local),
             dvalue.reshape(group_rows, width_local),
-        ]
-    ).astype(jnp.bfloat16)
-    grad_qkv = jnp.einsum("gd,cge->cde", slotted, dqkv, preferred_element_type=jnp.float32)
-    column_sums = jnp.sum(dqkv.astype(jnp.float32), axis=1)
-    resid_full = lax.dynamic_update_slice_in_dim(
-        jnp.zeros((group_rows, dfirst.shape[1]), jnp.float32), dfirst, row_start, 0
-    )
-    chosen = jnp.take(dqkv, slot_order, axis=1)
-    through = jnp.einsum("cge,cde->gd", chosen, qkv_weight, preferred_element_type=jnp.float32)
-    grad_tokens = lax.psum_scatter(
-        (through + jnp.take(resid_full, slot_order, axis=0)).astype(jnp.bfloat16),
-        "tensor",
-        scatter_dimension=0,
-        tiled=True,
-    ).astype(jnp.float32)
+        ],
+        axis=1,
+    ).astype(low)
+    grad_qkv = contract_rows(slotted, dqkv)
+    column_sums = jnp.sum(dqkv.astype(jnp.float32), axis=0).reshape(3, width_local)
+    through = times_transposed(dqkv, qkv_weight)
+    own_through = lax.dynamic_slice_in_dim(through, row_start, own_rows, 0) + dfirst
+    through = lax.dynamic_update_slice_in_dim(through, own_through, row_start, 0).astype(low)
+    leaving = leave_slots(slot_order, through)
     zero_row = jnp.zeros((bias_full.shape[1],), jnp.float32)
     grad_biases = jnp.stack(
         [
@@ -290,33 +738,25 @@
         ]
     )
     grad_gains = jnp.stack([grad_gain_one, grad_gain_two])
-    grad_proj, grad_gains, grad_biases, grad_upbias = (
-        lax.psum(grad_proj.astype(jnp.bfloat16), "tensor").astype(jnp.float32),
-        lax.psum(grad_gains.astype(jnp.bfloat16), "tensor").astype(jnp.float32),
-        lax.psum(grad_biases.astype(jnp.bfloat16), "tensor").astype(jnp.float32),
-        lax.psum(grad_upbias.astype(jnp.bfloat16), "tensor").astype(jnp.float32),
-    )
-    summed = (
-        lax.psum_scatter(grad_qkv, "dp", scatter_dimension=1, tiled=True),
-        lax.psum_scatter(grad_out, "dp", scatter_dimension=1, tiled=True),
-        lax.psum_scatter(grad_up, "dp", scatter_dimension=0, tiled=True),
-        lax.psum_scatter(grad_down, "dp", scatter_dimension=1, tiled=True),
-        lax.psum_scatter(grad_proj, "dp", scatter_dimension=0, tiled=True),
-        lax.psum_scatter(grad_gains, "dp", scatter_dimension=1, tiled=True),
-        lax.psum_scatter(grad_biases, "dp", scatter_dimension=1, tiled=True),
-        lax.psum_scatter(grad_upbias, "dp", scatter_dimension=0, tiled=True),
-    )
+    small_grad = jnp.concatenate([grad_gains, grad_biases]).reshape(8, size, part_rows).transpose(1, 0, 2)
+    small_grad = jnp.concatenate([small_grad, grad_upbias.reshape(size, -1, part_rows)], axis=1)
+    parts = [
+        grad.astype(low).reshape(size, part_rows, grad.shape[1])
+        for grad in (grad_qkv, grad_up, grad_out, grad_down, grad_proj)
+    ]
+    summed, grad_tokens = scatter_all([*parts, small_grad], 2, leaving, size, 7)
+    sum_qkv, sum_up, sum_out, sum_down, sum_proj, sum_small = summed
     return (
         embeddings,
         grad_tokens,
-        summed[0],
-        summed[1],
-        summed[2],
-        summed[3],
-        summed[4],
-        summed[5],
-        summed[6],
-        summed[7],
+        sum_qkv.reshape(part_rows, 3, width_local).transpose(1, 0, 2),
+        sum_out.T,
+        sum_up,
+        sum_down.T,
+        sum_proj,
+        sum_small[:2],
+        sum_small[2:8],
+        sum_small[8:].reshape(-1),
     )
 
 

time: 1150 us -> 627 us (0.55)
  waiting for transfers between devices: 512 us -> 0 us
  Pallas kernels: 0 us -> 273 us
  blocking collectives: 218 us -> 0 us
  local copies, waits for them, and re-layouts: 112 us -> 68.4 us
  between operations: 18 us -> 2.44 us
  matrix products: 189 us -> 176 us
    reduce_scatter x7 -> x0, waiting for transfers between devices: 306 us -> none  [the longest x1 73.1 us: body(): lax.psum_scatter(grad_down, 'dp', scatter_dimension=1, tiled=True)]
    pallas_call x0 -> x10, Pallas kernels: none -> 273 us  [the longest x3 73.6 us: scatter_rows(): pl.pallas_call(kernel, out_shape=jax.ShapeDtypeStruct(parts.shape[1:], jn...]
    all_gather x6 -> x0, blocking collectives: 170 us -> none  [the longest x1 36.3 us: body(): lax.all_gather(w_qkv.astype(jnp.bfloat16), 'dp', axis=1, tiled=True)]
    unnamed x22 -> x0, waiting for transfers between devices: 131 us -> none
    all_gather x6 -> x0, waiting for transfers between devices: 74.9 us -> none  [the longest x1 28.2 us: body(): dsecond_rows = lax.all_gather(dsecond_low, 'tensor', axis=0, tiled=True)]
    gather x3 -> x0, local copies, waits for them, and re-layouts: 44.7 us -> none  [the longest x1 18.9 us: body(): chosen = jnp.take(dqkv, slot_order, axis=1)]
    unnamed x1 -> x0, blocking collectives: 37.2 us -> none
    select_n x3 -> x0, other arithmetic: 11.8 us -> none  [the longest x1 9.68 us: body(): chosen = jnp.take(dqkv, slot_order, axis=1)]
  transfers between devices with their start and end apart: 18 -> 0, of which waited for: 13 -> 0; matrix products, arithmetic and copies ran while one was open for 24% -> 0% of each run, Pallas kernels for 0% -> 0%
where the time goes in v1:
time: 627 us; the launch traced here: 615 us
  Pallas kernels  273 us (44%)
  matrix products  176 us (28%)
  other arithmetic  79 us (13%)
  local copies, waits for them, and re-layouts  68.4 us (11%)
  loops' own time  16.3 us (3%)
    pallas_call x3, Pallas kernels, scatter_rows(): pl.pallas_call(kernel, out_shape=jax.ShapeDtypeStruct(parts.shape[1:], jn...  73.6 us
    pallas_call x3, Pallas kernels, gather_rows(): pl.pallas_call(kernel, out_shape=jax.ShapeDtypeStruct((4, *own.shape), ow...  70.2 us
    pallas_call x1, Pallas kernels, scatter_all(): pl.pallas_call(kernel, out_shape=[jax.ShapeDtypeStruct(p.shape[1:], f32)...  52.5 us
    pallas_call x1, Pallas kernels, gather_all(): pl.pallas_call(kernel, out_shape=[jax.ShapeDtypeStruct((size, *s.shape),...  49 us
    dot_general x4, matrix products, step(): jnp.einsum('hqk,khe->qhe', dscore, key_rows, preferred_element_type=jnp.f...  22.6 us
    dot_general x4, matrix products, step(): jnp.einsum('hqk,qhe->khe', soft_probs.astype(jnp.bfloat16), dout_block, p...  21.9 us
    dot_general x5, matrix products, times_transposed(): lax.dot_general(left, right, (((1,), (1,)), ((), ())), preferred_element_...  21.5 us
    convert_element_type x4, other arithmetic, step(): dscore = (soft_probs * (dsoft - jnp.sum(soft_probs * dsoft, axis=-1, keep...  19.9 us

profile of v1, /device:TPU:0, one launch (start us, length us, event | category | flops | bytes accessed | tf_op | source)
XLA Modules:
  0.0 615.2 jit_solution(6887506417191354793)
XLA Ops:
  17.1 49.0 %gather_all.1 = (bf16[8,96,576]{2,1,0:T(8,128)(2,1)}, bf16[8,96,768]{2,1,0:T(8,128)(2,1)}, bf16[8,96,192]{2,1,0:T(8,128)(2,1)}, bf16[8,96,768]{2,1,0:T(8,128)(2,...) custom-call(bf16[96,576]{1,0:T(8,128)(2,1)} %copy.39.refs_0_, ...), custom_call_target="tpu_custom_call" | custom-call | tf_op jit(solution)/shard_map/gather_all/pallas_call | solution.py:457
  71.7 16.7 %enter_slots.1 = (bf16[2048,768]{1,0:T(8,128)(2,1)}, bf16[2048,576]{1,0:T(8,128)(2,1)}) custom-call(s32[1,2048]{1,0:T(1,128)} %slots_ref.1, bf16[2048,768]{1,0:T(8,128)(2,1)} %bitcast.201, bf16[768,576]{1,0:T(8,128)(2,1)} %bitcast.216, f32[1,576]{1,0:T(1,128)} %reshape.316.shift_ref), custom_call_target="tpu_custom_call" | custom-call | tf_op jit(solution)/shard_map/enter_slots/pallas_call | solution.py:558
  88.4 3.9 fusion.66
  98.5 49.4 %while.44 = (s32[]{:T(128)}, bf16[4,512,3,64]{1,3,2,0:T(8,128)(2,1)S(1)}, f32[4,3,512]{2,1,0:T(4,128)}, s32[4]{0:T(128)S(1)}, bf16[1,4,512,3,64]{2,4,3,1,0:T(8,1...) while((s32[]{:T(128)}, ...), condition=%wide.region_3.4_spmd.clone, body=%wide.region_0.3_spmd.clone.sunk | while | flops 843055616 | bytes 39975208 | solution.py:66
  103.8 2.8 fusion.118
  106.6 3.7 fusion.119
  116.1 2.8 fusion.118
  118.9 3.7 fusion.119
  128.5 2.8 fusion.118
  131.3 3.7 fusion.119
  140.8 2.8 fusion.118
  143.6 3.7 fusion.119
  149.6 2.7 convolution_convert_fusion.2
  152.4 24.5 %scatter_rows.3 = f32[512,768]{1,0:T(8,128)} custom-call(bf16[4,512,768]{2,1,0:T(8,128)(2,1)} %bitcast.188), custom_call_target="tpu_custom_call" | custom-call | tf_op jit(solution)/shard_map/scatter_rows/pallas_call | solution.py:416
  180.9 23.5 %gather_rows.3 = bf16[4,512,768]{2,1,0:T(8,128)(2,1)} custom-call(bf16[512,768]{1,0:T(8,128)(2,1)} %fusion.53.own_ref), custom_call_target="tpu_custom_call" | custom-call | tf_op jit(solution)/shard_map/gather_rows/pallas_call | solution.py:390
  204.4 19.1 %multiply_convert_fusion.1 = (bf16[2048,768]{1,0:T(8,128)(2,1)S(1)}, f32[2048,768]{1,0:T(8,128)}, f32[2048,768]{1,0:T(8,128)}) fusion(f32[768]{0:T(1024)S(1)} %copy-done.41, bf16[2048,768]{1,0:T(8,128)(2,1)} %bitcast.199, bf16[768,768]{1,0:T(8,128)(2,1)} %bitcast.229), kind=kOutput, calls=%fused_computation.56 | convolution fusion | flops 2519728128 | bytes 20057088 | tf_op jit(solution)/shard_map/dot_general | solution.py:665
  223.5 4.0 convolution_convert_fusion.1
  227.5 24.5 %scatter_rows.4 = f32[512,768]{1,0:T(8,128)} custom-call(bf16[4,512,768]{2,1,0:T(8,128)(2,1)} %bitcast.193), custom_call_target="tpu_custom_call" | custom-call | tf_op jit(solution)/shard_map/scatter_rows/pallas_call | solution.py:416
  259.5 4.0 multiply_reduce_fusion.1
  265.6 3.5 fusion.62
  270.5 3.1 add_reduce_fusion.1
  274.9 23.3 %gather_rows.4 = bf16[4,512,768]{2,1,0:T(8,128)(2,1)} custom-call(bf16[512,768]{1,0:T(8,128)(2,1)} %get-tuple-element.548.own_ref), custom_call_target="tpu_custom_call" | custom-call | tf_op jit(solution)/shard_map/gather_rows/pallas_call | solution.py:390
  298.3 10.5 %convert_reduce_fusion = (f32[768]{0:T(1024)S(1)}, bf16[2048,768]{1,0:T(8,128)(2,1)S(1)}) fusion(f32[2048,768]{1,0:T(8,128)} %get-tuple-element.535, f32[2048,768]{1,0:T(8,128)} %get-tuple-element.555, f32[768]{0:T(1024)} %dynamic_slice.74, bf16[2048,768]{1,0:T(8,128)(2,1)} %bitcast.202, bf16[768,768]{1,0:T(8,128)(2,1)} %bitcast.231), kind=kOutput, calls=%fused_computation.54 | convolution fusion | flops 2442657024 | bytes 20060160 | tf_op jit(solution)/shard_map/dot_general | solution.py:688
  308.9 3.9 convolution_convert_fusion.4
  312.8 4.0 convolution_convert_fusion.5
  320.2 6.6 %convolution_convert_fusion = bf16[2048,768]{1,0:T(8,128)(2,1)} fusion(bf16[2048,768]{1,0:T(8,128)(2,1)} %copy-done.46, bf16[768,768]{1,0:T(8,128)(2,1)} %bitcast.230), kind=kOutput, calls=%fused_computation.71 | convolution fusion | flops 2417491968 | bytes 7471104 | tf_op jit(solution)/shard_map/dot_general | solution.py:36
  326.7 24.6 %scatter_rows.5 = f32[512,768]{1,0:T(8,128)} custom-call(bf16[4,512,768]{2,1,0:T(8,128)(2,1)} %bitcast.192), custom_call_target="tpu_custom_call" | custom-call | tf_op jit(solution)/shard_map/scatter_rows/pallas_call | solution.py:416
  351.3 4.3 multiply_reduce_fusion.2
  357.7 3.1 fusion.61
  361.4 2.6 add_convert_fusion.2.own_ref
  364.0 23.3 %gather_rows.5 = bf16[4,512,768]{2,1,0:T(8,128)(2,1)} custom-call(bf16[512,768]{1,0:T(8,128)(2,1)} %add_convert_fusion.2.own_ref), custom_call_target="tpu_custom_call" | custom-call | tf_op jit(solution)/shard_map/gather_rows/pallas_call | solution.py:390
  387.4 3.5 convolution_convert_fusion.7
  393.0 3.0 reshape.331
  399.2 120.3 %while.45 = (s32[]{:T(128)}, f32[2048,3,64]{0,2,1:T(8,128)S(1)}, f32[2048,3,64]{0,2,1:T(8,128)}, bf16[4,512,3,64]{1,3,2,0:T(8,128)(2,1)}, s32[4]{0:T(128)S(1)}, ...) while((s32[]{:T(128)}, f32[2048,3,64]{0,2,1:T(8,128)S(1)}, ...), condition=%wide.region_16.17_spmd.clone, body=%wide.region_14.16_spmd.clone.sunk | while | flops 2062516736 | bytes 129419512 | solution.py:117
  403.3 2.7 fusion.129
  406.1 5.0 fusion.131
  411.1 4.8 multiply_reduce_fusion.10
  415.9 5.0 multiply_convert_fusion.3
  420.9 5.7 fusion.132
  426.6 2.3 fusion.130
  432.9 2.7 fusion.129
  435.6 5.6 fusion.131
  441.2 4.8 multiply_reduce_fusion.10
  446.1 5.0 multiply_convert_fusion.3
  451.0 5.6 fusion.132
  456.7 2.3 fusion.130
  463.0 2.7 fusion.129
  465.7 5.6 fusion.131
  471.3 4.8 multiply_reduce_fusion.10
  476.2 5.0 multiply_convert_fusion.3
  481.2 5.6 fusion.132
  486.8 2.3 fusion.130
  493.1 2.7 fusion.129
  495.8 5.6 fusion.131
  501.5 4.8 multiply_reduce_fusion.10
  506.3 5.0 multiply_convert_fusion.3
  511.3 5.6 fusion.132
  516.9 2.3 fusion.130
  525.2 2.9 convolution_convert_fusion.6
  529.1 2.2 copy.51
  531.4 4.2 fusion.60
  538.1 11.1 %leave_slots.1 = bf16[2048,768]{1,0:T(8,128)(2,1)} custom-call(s32[2048,1]{1,0:T(8,128)} %copy.53.slots_ref, bf16[2048,768]{1,0:T(8,128)(2,1)} %convert_element_type.157.rows_ref), custom_call_target="tpu_custom_call" | custom-call | tf_op jit(solution)/shard_map/leave_slots/pallas_call | solution.py:585
  550.0 52.5 %scatter_all.1 = (f32[96,576]{1,0:T(8,128)}, f32[96,768]{1,0:T(8,128)}, f32[96,192]{1,0:T(8,128)}, f32[96,768]{1,0:T(8,128)}, f32[96,128]{1,0:T(8,128)}, /*index=5*/f32[12,96]{1,0:T(8,128)}, f32[512,768]{1,0:T(8,128)}) custom-call(bf16[8,96,576]{2,1,0:T(8,128)(2,1)} %bitcast.191, bf16[8,96,768]{2,1,0:T(8,128)(2,1)} %bitcast.214, ...), custom_call_target="tpu_custom_call" | custom-call | tf_op jit(solution)/shard_map/scatter_all/pallas_call | solution.py:527
  610.0 2.7 copy.93
  (235 shorter events, 99.6 us)
Async XLA Ops:
  69.3 110.4 %copy-start.25 = (f32[768]{0:T(1024)}, f32[768]{0:T(1024)S(1)}, u32[]{:S(2)}) copy-start(f32[768]{0:T(1024)S(1)} %add.223) | copy-start | bytes 9220
  147.9 4.5 copy-start.4
  147.9 1.7 copy-start.12
  148.7 0.9 copy-start.6
  179.1 0.5 copy-start.28
  180.9 23.5 %copy-start.41 = (f32[768]{0:T(1024)S(1)}, f32[768]{0:T(1024)}, u32[]{:S(2)}) copy-start(f32[768]{0:T(1024)} %dynamic_slice.74) | copy-start | bytes 9220
  204.4 19.1 %copy-start.42 = (bf16[8,96,768]{2,1,0:T(8,128)(2,1)S(1)}, bf16[8,96,768]{2,1,0:T(8,128)(2,1)}, u32[]{:S(2)}) copy-start(bf16[8,96,768]{2,1,0:T(8,128)(2,1)} %get-tuple-element.342) | copy-start | bytes 3538948
  223.5 4.0 copy-start.44
  252.1 2.4 copy-start.22
  252.1 2.4 copy-start.34
  254.1 3.7 copy-start.2
  254.1 1.1 copy-start.15
  254.1 1.3 copy-start.17
  254.1 1.3 copy-start.27
  254.1 1.7 copy-start.23
  254.4 1.4 copy-start.30
  254.5 1.4 copy-start.26
  256.7 1.1 copy-start.14
  269.1 29.2 %copy-start.33 = (f32[512]{0:T(512)}, f32[512]{0:T(512)S(1)}, u32[]{:S(2)}) copy-start(f32[512]{0:T(512)S(1)} %negate_multiply_fusion.2) | copy-start | bytes 6148
  298.3 10.6 %copy-start.10 = (bf16[4,512,768]{2,1,0:T(8,128)(2,1)S(1)}, bf16[4,512,768]{2,1,0:T(8,128)(2,1)}, u32[]{:S(2)}) copy-start(bf16[4,512,768]{2,1,0:T(8,128)(2,1)} %gather_rows.4) | copy-start | bytes 9437188
  298.3 10.6 %copy-start.45 = (bf16[2048,768]{1,0:T(8,128)(2,1)S(1)}, bf16[2048,768]{1,0:T(8,128)(2,1)}, u32[]{:S(2)}) copy-start(bf16[2048,768]{1,0:T(8,128)(2,1)} %copy-done.44) | copy-start | bytes 9437188
  308.9 3.9 copy-start.46
  308.9 3.9 copy-start.9
  351.3 5.7 copy-start.29
  357.7 3.1 copy-start.40
  360.8 26.6 %copy-start.31 = (f32[512]{0:T(512)}, f32[512]{0:T(512)S(1)}, u32[]{:S(2)}) copy-start(f32[512]{0:T(512)S(1)} %negate_multiply_fusion.1) | copy-start | bytes 6148
  361.4 25.9 %copy-start.7 = (bf16[24,8,4,512]{3,1,2,0:T(8,128)(2,1)S(1)}, bf16[24,8,4,512]{3,1,2,0:T(8,128)(2,1)}, u32[]{:S(2)}) copy-start(bf16[24,8,4,512]{3,1,2,0:T(8,128)(2,1)} %copy-done.6) | copy-start | bytes 2359300
  387.4 3.6 copy-start.3
  390.9 8.3 %copy-start.1 = (f32[2048,3,64]{0,2,1:T(8,128)S(1)}, f32[2048,3,64]{0,2,1:T(8,128)}, u32[]{:S(2)}) copy-start(f32[2048,3,64]{0,2,1:T(8,128)} %custom-call) | copy-start | bytes 4718596
  390.9 8.3 %copy-start.43 = (s32[4]{0:T(128)S(1)}, s32[4]{0:T(128)}, u32[]{:S(2)}) copy-start(s32[4]{0:T(128)} %iota.22) | copy-start | bytes 52
  420.9 5.7 copy-start
  451.0 5.6 copy-start
  481.2 5.6 copy-start
  511.3 5.6 copy-start
  519.5 2.0 copy-start.13
  521.5 6.6 %copy-start.8 = (bf16[24,8,4,512]{3,1,2,0:T(8,128)(2,1)}, bf16[24,8,4,512]{3,1,2,0:T(8,128)(2,1)S(1)}, u32[]{:S(2)}) copy-start(bf16[24,8,4,512]{3,1,2,0:T(8,128)(2,1)S(1)} %copy.59) | copy-start | bytes 2359300
  522.6 2.6 copy-start.20
  522.7 5.5 copy-start.11
  528.1 3.2 copy-start.16
  531.3 4.2 copy-start.5
  531.3 4.2 copy-start.32
  538.0 11.2 %copy-start.35 = (f32[1,8,96]{2,0,1:T(1,128)S(1)}, f32[1,8,96]{2,0,1:T(1,128)}, u32[]{:S(2)}) copy-start(f32[1,8,96]{2,0,1:T(1,128)} %concatenate.37) | copy-start | bytes 9220
  538.0 11.2 %copy-start.36 = (f32[1,8,96]{2,0,1:T(1,128)S(1)}, f32[1,8,96]{2,0,1:T(1,128)}, u32[]{:S(2)}) copy-start(f32[1,8,96]{2,0,1:T(1,128)} %concatenate.43) | copy-start | bytes 9220
  538.0 11.2 %copy-start.37 = (f32[1,8,96]{2,0,1:T(1,128)S(1)}, f32[1,8,96]{2,0,1:T(1,128)}, u32[]{:S(2)}) copy-start(f32[1,8,96]{2,0,1:T(1,128)} %concatenate.42) | copy-start | bytes 9220
  538.0 11.2 %copy-start.38 = (f32[1,8,96]{2,0,1:T(1,128)S(1)}, f32[1,8,96]{2,0,1:T(1,128)}, u32[]{:S(2)}) copy-start(f32[1,8,96]{2,0,1:T(1,128)} %concatenate.36) | copy-start | bytes 9220
  538.0 11.2 %copy-start.39 = (f32[1,8,96]{2,0,1:T(1,128)S(1)}, f32[1,8,96]{2,0,1:T(1,128)}, u32[]{:S(2)}) copy-start(f32[1,8,96]{2,0,1:T(1,128)} %concatenate.41) | copy-start | bytes 9220
  538.1 11.3 %copy-start.21 = (f32[8,4,96]{2,1,0:T(4,128)S(1)}, f32[8,4,96]{2,1,0:T(4,128)}, u32[]{:S(2)}) copy-start(f32[8,4,96]{2,1,0:T(4,128)} %reshape.340) | copy-start | bytes 36868
  602.5 10.2 %copy-start.19 = (f32[96,768]{1,0:T(8,128)S(1)}, f32[96,768]{1,0:T(8,128)}, u32[]{:S(2)}) copy-start(f32[96,768]{1,0:T(8,128)} %get-tuple-element.774) | copy-start | bytes 884740
  602.5 10.9 %copy-start.18 = (f32[96,768]{1,0:T(8,128)S(1)}, f32[96,768]{1,0:T(8,128)}, u32[]{:S(2)}) copy-start(f32[96,768]{1,0:T(8,128)} %get-tuple-element.352) | copy-start | bytes 884740
  602.5 11.6 %copy-start.24 = (f32[96,128]{1,0:T(8,128)S(1)}, f32[96,128]{1,0:T(8,128)}, u32[]{:S(2)}) copy-start(f32[96,128]{1,0:T(8,128)} %get-tuple-element.776) | copy-start | bytes 147460

commit v2 on v1

--- a/solution.py
+++ b/solution.py
@@ -38,92 +38,184 @@
     )
 
 
-def attend(query_heads, key_heads, value_heads, key_mask, num_blocks, factor):
-
-    def one_block(position):
-        passage_idx = position // num_blocks
-        block_idx = position % num_blocks
-        query_block = query_heads[passage_idx, block_idx]
-        scores = (
-            jnp.einsum(
-                "qhe,khe->hqk",
-                query_block,
-                key_heads[passage_idx],
-                preferred_element_type=jnp.float32,
-            )
-            * factor
-        )
-        scores = jnp.where(key_mask[passage_idx][None, None, :], scores, NEG_FILL)
-        row_top = jnp.max(scores, axis=-1, keepdims=True)
-        shifted = jnp.exp(scores - row_top)
-        row_total = jnp.sum(shifted, axis=-1, keepdims=True)
-        soft_low = (shifted / row_total).astype(jnp.bfloat16)
-        result = jnp.einsum(
-            "hqk,khe->qhe", soft_low, value_heads[passage_idx], preferred_element_type=jnp.float32
-        )
-        return (result, (row_top + jnp.log(row_total))[..., 0])
-
-    return lax.map(one_block, jnp.arange(query_heads.shape[0] * num_blocks))
-
-
-def attend_back(
-    query_heads, key_heads, value_heads, dcontext_heads, log_total, key_mask, num_blocks, factor
-):
-
-    def passage(passage_idx):
-        key_rows = key_heads[passage_idx]
-        value_rows = value_heads[passage_idx]
-        mask_row = key_mask[passage_idx][None, None, :]
-
-        def step(carry, block_idx):
-            dkey_sum, dvalue_sum = carry
-            query_block = query_heads[passage_idx, block_idx]
-            dout_block = dcontext_heads[passage_idx, block_idx]
-            total_block = log_total[passage_idx * num_blocks + block_idx]
-            scores = (
-                jnp.einsum(
-                    "qhe,khe->hqk", query_block, key_rows, preferred_element_type=jnp.float32
-                )
-                * factor
-            )
-            scores = jnp.where(mask_row, scores, NEG_FILL)
-            soft_probs = jnp.exp(scores - total_block[..., None])
-            dvalue_sum = dvalue_sum + jnp.einsum(
-                "hqk,qhe->khe",
-                soft_probs.astype(jnp.bfloat16),
-                dout_block,
-                preferred_element_type=jnp.float32,
-            )
-            dsoft = jnp.einsum(
-                "qhe,khe->hqk", dout_block, value_rows, preferred_element_type=jnp.float32
-            )
-            dscore = (
-                soft_probs * (dsoft - jnp.sum(soft_probs * dsoft, axis=-1, keepdims=True))
-            ).astype(jnp.bfloat16)
-            dquery = (
-                jnp.einsum("hqk,khe->qhe", dscore, key_rows, preferred_element_type=jnp.float32)
-                * factor
-            )
-            dkey_sum = (
-                dkey_sum
-                + jnp.einsum(
-                    "hqk,qhe->khe", dscore, query_block, preferred_element_type=jnp.float32
-                )
-                * factor
-            )
-            return ((dkey_sum, dvalue_sum), dquery)
-
-        zero_grad = jnp.zeros(key_rows.shape, jnp.float32)
-        (dkey_sum, dvalue_sum), dquery = lax.scan(
-            step, (zero_grad, zero_grad), jnp.arange(num_blocks)
-        )
-        return (dquery, dkey_sum, dvalue_sum)
-
-    return lax.map(passage, jnp.arange(key_heads.shape[0]))
-
-
 MESH = pl.DeviceIdType.MESH
 VMEM = pl.BlockSpec(memory_space=pltpu.VMEM)
+WIDE = 128
+
+
+def lane_index(rows):
+    return lax.broadcasted_iota(jnp.int32, (rows, WIDE - HEAD_DIM), 1)
+
+
+def thirds(column):
+    parts = []
+    for _ in range(3):
+        part = column.astype(jnp.bfloat16).astype(jnp.float32)
+        parts.append(part)
+        column = column - part
+    return parts
+
+
+def beside(rows, columns):
+    lane = lane_index(rows)
+    out = jnp.zeros(lane.shape, jnp.float32)
+    for i, column in enumerate(columns):
+        out = jnp.where(lane == i, column, out)
+    return out.astype(jnp.bfloat16)
+
+
+def key_fill(length, keys):
+    position = lax.broadcasted_iota(jnp.int32, (keys, 1), 0)
+    return jnp.where(position < length, 0.0, NEG_FILL)
+
+
+def attend(qkv, lengths, passages):
+    rows, width = qkv.shape[0], qkv.shape[1] // 3
+    keys, heads = rows // passages, width // HEAD_DIM
+    block = 512
+    steps = keys // block
+    factor = HEAD_DIM ** (-0.5)
+
+    def kernel(len_ref, query_ref, kv_ref, out_ref, exact_ref, total_ref, key_side, value_side):
+        passage, step = pl.program_id(0), pl.program_id(1)
+
+        @pl.when(step == 0)
+        def _():
+            fill = key_fill(len_ref[passage], keys)
+            for h in range(heads):
+                at = width + h * HEAD_DIM
+                key_side[h, :, :HEAD_DIM] = kv_ref[:, at : at + HEAD_DIM]
+                key_side[h, :, HEAD_DIM:] = beside(keys, [fill])
+                value_side[h, :, :HEAD_DIM] = kv_ref[:, at + width : at + width + HEAD_DIM]
+                value_side[h, :, HEAD_DIM:] = beside(keys, [1.0])
+
+        ones = beside(block, [1.0])
+        totals = jnp.zeros((block, WIDE), jnp.float32)
+        lane = lax.broadcasted_iota(jnp.int32, (block, WIDE), 1)
+        for h in range(heads):
+            query = query_ref[:, h * HEAD_DIM : (h + 1) * HEAD_DIM] * jnp.bfloat16(factor)
+            query = jnp.concatenate([query, ones], axis=1)
+            scores = lax.dot_general(
+                query, key_side[h], (((1,), (1,)), ((), ())), preferred_element_type=jnp.float32
+            )
+            top = jnp.max(scores, axis=-1, keepdims=True)
+            soft = jnp.exp(scores - top).astype(jnp.bfloat16)
+            mixed = jnp.dot(soft, value_side[h], preferred_element_type=jnp.float32)
+            total = mixed[:, HEAD_DIM : HEAD_DIM + 1]
+            result = mixed[:, :HEAD_DIM] / total
+            exact_ref[:, h * HEAD_DIM : (h + 1) * HEAD_DIM] = result
+            out_ref[:, h * HEAD_DIM : (h + 1) * HEAD_DIM] = result.astype(jnp.bfloat16)
+            totals = jnp.where(lane == h, top + jnp.log(total), totals)
+        total_ref[...] = totals
+
+    def tile(columns):
+        return pl.BlockSpec((block, columns), lambda p, i: (p * steps + i, 0))
+
+    return pl.pallas_call(
+        kernel,
+        grid=(passages, steps),
+        in_specs=[
+            pl.BlockSpec(memory_space=pltpu.SMEM),
+            tile(3 * width),
+            pl.BlockSpec((keys, 3 * width), lambda p, i: (p, 0)),
+        ],
+        out_specs=[tile(width), tile(width), tile(WIDE)],
+        out_shape=[
+            jax.ShapeDtypeStruct((rows, width), jnp.bfloat16),
+            jax.ShapeDtypeStruct((rows, width), jnp.float32),
+            jax.ShapeDtypeStruct((rows, WIDE), jnp.float32),
+        ],
+        scratch_shapes=[pltpu.VMEM((heads, keys, WIDE), jnp.bfloat16)] * 2,
+        name="attend",
+    )(lengths, qkv, qkv)
+
+
+def attend_back(qkv, dcontext, exact, totals, lengths, passages):
+    rows, width = qkv.shape[0], qkv.shape[1] // 3
+    keys, heads = rows // passages, width // HEAD_DIM
+    block = 512
+    steps = keys // block
+    factor = HEAD_DIM ** (-0.5)
+
+    def kernel(
+        len_ref, query_ref, dout_ref, exact_ref, total_ref, kv_ref, out_ref, key_side, value_side, key_turned, sums
+    ):
+        passage, step = pl.program_id(0), pl.program_id(1)
+
+        @pl.when(step == 0)
+        def _():
+            fill = key_fill(len_ref[passage], keys)
+            for h in range(heads):
+                at = width + h * HEAD_DIM
+                key = kv_ref[:, at : at + HEAD_DIM]
+                key_side[h, :, :HEAD_DIM] = key
+                key_side[h, :, HEAD_DIM:] = beside(keys, [fill, 1.0, 1.0, 1.0])
+                key_turned[h] = (key * jnp.bfloat16(factor)).T
+                value_side[h, :, :HEAD_DIM] = kv_ref[:, at + width : at + width + HEAD_DIM]
+                value_side[h, :, HEAD_DIM:] = beside(keys, [1.0, 1.0, 1.0])
+            sums[...] = jnp.zeros_like(sums)
+
+        first = pl.multiple_of(step * block, block)
+        blank = jnp.zeros((block, HEAD_DIM), jnp.bfloat16)
+        for h in range(heads):
+            lanes = slice(h * HEAD_DIM, (h + 1) * HEAD_DIM)
+            dout = dout_ref[:, lanes]
+            delta = jnp.sum(dout.astype(jnp.float32) * exact_ref[:, lanes], axis=-1, keepdims=True)
+            query = query_ref[:, lanes] * jnp.bfloat16(factor)
+            query_wide = jnp.concatenate(
+                [query, beside(block, [1.0, *thirds(-total_ref[:, h : h + 1])])], axis=1
+            )
+            dout_wide = jnp.concatenate([dout, beside(block, thirds(-delta))], axis=1)
+            nt = (((1,), (1,)), ((), ()))
+            soft = jnp.exp(
+                lax.dot_general(key_side[h], query_wide, nt, preferred_element_type=jnp.float32)
+            )
+            dsoft = lax.dot_general(value_side[h], dout_wide, nt, preferred_element_type=jnp.float32)
+            dscore = (soft * dsoft).astype(jnp.bfloat16)
+            soft = soft.astype(jnp.bfloat16)
+            sums[h] += jnp.dot(
+                soft, jnp.concatenate([dout, blank], axis=1), preferred_element_type=jnp.float32
+            ) + jnp.dot(
+                dscore, jnp.concatenate([blank, query], axis=1), preferred_element_type=jnp.float32
+            )
+            dquery = jnp.dot(key_turned[h], dscore, preferred_element_type=jnp.float32)
+            out_ref[pl.ds(first, block), lanes] = dquery.T.astype(jnp.bfloat16)
+
+        @pl.when(step == steps - 1)
+        def _():
+            for h in range(heads):
+                both = sums[h].astype(jnp.bfloat16)
+                at = width + h * HEAD_DIM
+                out_ref[:, at : at + HEAD_DIM] = both[:, HEAD_DIM:]
+                out_ref[:, at + width : at + width + HEAD_DIM] = both[:, :HEAD_DIM]
+
+    def tile(columns):
+        return pl.BlockSpec((block, columns), lambda p, i: (p * steps + i, 0))
+
+    whole = pl.BlockSpec((keys, 3 * width), lambda p, i: (p, 0))
+    return pl.pallas_call(
+        kernel,
+        grid=(passages, steps),
+        in_specs=[
+            pl.BlockSpec(memory_space=pltpu.SMEM),
+            tile(3 * width),
+            tile(width),
+            tile(width),
+            tile(WIDE),
+            whole,
+        ],
+        out_specs=whole,
+        out_shape=jax.ShapeDtypeStruct((rows, 3 * width), jnp.bfloat16),
+        scratch_shapes=[
+            pltpu.VMEM((heads, keys, WIDE), jnp.bfloat16),
+            pltpu.VMEM((heads, keys, WIDE), jnp.bfloat16),
+            pltpu.VMEM((heads, HEAD_DIM, keys), jnp.bfloat16),
+            pltpu.VMEM((heads, keys, WIDE), jnp.float32),
+        ],
+        name="attend_back",
+    )(lengths, qkv, dcontext, exact, totals, qkv)
+
+
 RING_MAX = 8
 ROW_PIECES = 4
 
@@ -611,9 +703,6 @@
     own_rows = tokens.shape[0]
     group_rows = own_rows * tensor_size
     passages = group_rows // SLOT
-    block_rows = min(512, SLOT)
-    num_blocks = SLOT // block_rows
-    factor = HEAD_DIM ** (-0.5)
     slot_order = arrival_slots[0]
     size = lax.axis_size("dp")
     part_rows, width_local = w_qkv.shape[1:]
@@ -648,14 +737,7 @@
     resid_input = lax.dynamic_slice_in_dim(slotted, row_start, own_rows, 0).astype(jnp.float32)
     positions = row_start + jnp.arange(own_rows, dtype=jnp.int32)
     row_keep = (positions % SLOT < lengths[positions // SLOT]).astype(jnp.float32)
-    key_mask = jnp.arange(SLOT, dtype=jnp.int32)[None, :] < lengths[:, None]
-    block_shape = (passages, num_blocks, block_rows, heads_local, HEAD_DIM)
-    slot_shape = (passages, SLOT, heads_local, HEAD_DIM)
-    query_heads = qkv_all[:, 0 * width_local : 1 * width_local].reshape(block_shape)
-    key_heads = qkv_all[:, 1 * width_local : 2 * width_local].reshape(slot_shape)
-    value_heads = qkv_all[:, 2 * width_local : 3 * width_local].reshape(slot_shape)
-    attended, log_total = attend(query_heads, key_heads, value_heads, key_mask, num_blocks, factor)
-    context = attended.reshape(group_rows, width_local).astype(jnp.bfloat16)
+    context, exact, totals = attend(qkv_all, lengths, passages)
     attn_part = scatter_rows(times_transposed(context, out_weight).astype(low), 1)
     first_sum = resid_input + attn_part + bias_full[2]
     first_norm, back_first = jax.vjp(norm_rows, first_sum, gain_full[0], bias_full[3])
@@ -702,24 +784,7 @@
     dfirst_rows = gather_rows(dfirst_low, 6)
     dcontext = jnp.dot(dfirst_rows, out_weight, preferred_element_type=jnp.float32).astype(low)
     grad_out = contract_rows(dfirst_rows, context)
-    dquery, dkey, dvalue = attend_back(
-        query_heads,
-        key_heads,
-        value_heads,
-        dcontext.reshape(block_shape),
-        log_total,
-        key_mask,
-        num_blocks,
-        factor,
-    )
-    dqkv = jnp.concatenate(
-        [
-            dquery.reshape(group_rows, width_local),
-            dkey.reshape(group_rows, width_local),
-            dvalue.reshape(group_rows, width_local),
-        ],
-        axis=1,
-    ).astype(low)
+    dqkv = attend_back(qkv_all, dcontext, exact, totals, lengths, passages)
     grad_qkv = contract_rows(slotted, dqkv)
     column_sums = jnp.sum(dqkv.astype(jnp.float32), axis=0).reshape(3, width_local)
     through = times_transposed(dqkv, qkv_weight)

time: 627 us -> 493 us (0.79)
  matrix products: 176 us -> 73 us
  Pallas kernels: 273 us -> 337 us
  other arithmetic: 79 us -> 34.9 us
  local copies, waits for them, and re-layouts: 68.4 us -> 36.1 us
  loops' own time: 16.3 us -> 0 us
    dot_general x28 -> x0, matrix products: 107 us -> none  [the longest x4 22.6 us: step(): jnp.einsum('hqk,khe->qhe', dscore, key_rows, preferred_element_type=jnp.f...]
    pallas_call x0 -> x2, Pallas kernels: none -> 64.4 us  [the longest x1 40.2 us: attend_back(): pl.pallas_call(kernel, grid=(passages, steps), in_specs=[pl.BlockSpec(mem...]
    convert_element_type x4 -> x0, other arithmetic: 19.9 us -> none  [step(): dscore = (soft_probs * (dsoft - jnp.sum(soft_probs * dsoft, axis=-1, keep...]
    another operation x2 -> x0, loops' own time: 16.3 us -> none  [the longest x1 8.38 us: passage(): lax.scan(step, (zero_grad, zero_grad), jnp.arange(num_blocks))]
    reduce_sum x4 -> x0, other arithmetic: 11.2 us -> none  [one_block(): row_total = jnp.sum(shifted, axis=-1, keepdims=True)]
    slice x4 -> x0, local copies, waits for them, and re-layouts: 7.32 us -> none  [the longest x2 5.37 us: body(): qkv_all[:, 2 * width_local:3 * width_local].reshape(slot_shape)]
    unnamed x105 -> x81, local copies, waits for them, and re-layouts: 19 us -> 18.2 us
where the time goes in v2:
time: 493 us; the launch traced here: 483 us
  Pallas kernels  337 us (68%)
  matrix products  73 us (15%)
  local copies, waits for them, and re-layouts  36.1 us (7%)
  other arithmetic  34.9 us (7%)
    pallas_call x3, Pallas kernels, scatter_rows(): pl.pallas_call(kernel, out_shape=jax.ShapeDtypeStruct(parts.shape[1:], jn...  73.8 us
    pallas_call x3, Pallas kernels, gather_rows(): pl.pallas_call(kernel, out_shape=jax.ShapeDtypeStruct((4, *own.shape), ow...  70.2 us
    pallas_call x1, Pallas kernels, scatter_all(): pl.pallas_call(kernel, out_shape=[jax.ShapeDtypeStruct(p.shape[1:], f32)...  52.3 us
    pallas_call x1, Pallas kernels, gather_all(): pl.pallas_call(kernel, out_shape=[jax.ShapeDtypeStruct((size, *s.shape),...  48.8 us
    pallas_call x1, Pallas kernels, attend_back(): pl.pallas_call(kernel, grid=(passages, steps), in_specs=[pl.BlockSpec(mem...  40.2 us
    pallas_call x1, Pallas kernels, attend(): pl.pallas_call(kernel, grid=(passages, steps), in_specs=[pl.BlockSpec(mem...  24.2 us
    dot_general x5, matrix products, contract_rows(): lax.dot_general(left, right, (((0,), (0,)), ((), ())), preferred_element_...  20 us
    dot_general x5, matrix products, times_transposed(): lax.dot_general(left, right, (((1,), (1,)), ((), ())), preferred_element_...  19 us

profile of v2, /device:TPU:0, one launch (start us, length us, event | category | flops | bytes accessed | tf_op | source)
XLA Modules:
  0.0 483.4 jit_solution(6663627709275046847)
XLA Ops:
  0.6 1.7 copy.46
  3.6 1.0 convert_bitcast_fusion.1
  4.7 0.8 copy.45.refs_0_
  5.5 1.6 convert_element_type.98.refs_1_
  7.1 1.6 copy.44
  8.7 1.6 convert_bitcast_fusion.refs_3_
  10.4 1.4 convert_element_type.101.refs_4_
  14.5 48.8 %gather_all.1 = (bf16[8,96,576]{2,1,0:T(8,128)(2,1)}, bf16[8,96,768]{2,1,0:T(8,128)(2,1)}, bf16[8,96,192]{2,1,0:T(8,128)(2,1)}, bf16[8,96,768]{2,1,0:T(8,128)(2,...) custom-call(bf16[96,576]{1,0:T(8,128)(2,1)} %copy.45.refs_0_, ...), custom_call_target="tpu_custom_call" | custom-call | tf_op jit(solution)/shard_map/gather_all/pallas_call | solution.py:549
  63.4 0.8 convert_element_type.105
  65.4 0.7 slice.88
  67.4 16.7 %enter_slots.1 = (bf16[2048,768]{1,0:T(8,128)(2,1)}, bf16[2048,576]{1,0:T(8,128)(2,1)}) custom-call(s32[1,2048]{1,0:T(1,128)} %slots_ref.1, bf16[2048,768]{1,0:T(8,128)(2,1)} %bitcast.76, bf16[768,576]{1,0:T(8,128)(2,1)} %bitcast.85, f32[1,576]{1,0:T(1,128)} %reshape.234.shift_ref), custom_call_target="tpu_custom_call" | custom-call | tf_op jit(solution)/shard_map/enter_slots/pallas_call | solution.py:650
  84.1 24.2 %attend.1 = (bf16[2048,192]{1,0:T(8,128)(2,1)}, f32[2048,192]{1,0:T(8,128)}, f32[2048,128]{1,0:T(8,128)}) custom-call(s32[1]{0:T(128)} %copy.63.len_ref, bf16[2048,576]{1,0:T(8,128)(2,1)} %get-tuple-element.33.query_ref.kv_ref, bf16[2048,576]{1,0:T(8,128)(2,1)} %get-tuple-element.33.query_ref.kv_ref), custom_call_target="tpu_custom_call" | custom-call | tf_op jit(solution)/shard_map/attend/pallas_call | solution.py:114
  108.3 3.9 convolution_convert_fusion.2
  112.2 24.5 %scatter_rows.3 = f32[512,768]{1,0:T(8,128)} custom-call(bf16[4,512,768]{2,1,0:T(8,128)(2,1)} %bitcast.68), custom_call_target="tpu_custom_call" | custom-call | tf_op jit(solution)/shard_map/scatter_rows/pallas_call | solution.py:508
  136.7 1.9 fusion.17
  139.6 1.2 fusion.6.own_ref
  140.8 23.5 %gather_rows.3 = bf16[4,512,768]{2,1,0:T(8,128)(2,1)} custom-call(bf16[512,768]{1,0:T(8,128)(2,1)} %fusion.6.own_ref), custom_call_target="tpu_custom_call" | custom-call | tf_op jit(solution)/shard_map/gather_rows/pallas_call | solution.py:482
  164.4 18.7 %multiply_convert_fusion = (bf16[2048,768]{1,0:T(8,128)(2,1)S(1)}, f32[2048,768]{1,0:T(8,128)}, f32[2048,768]{1,0:T(8,128)}) fusion(f32[768]{0:T(1024)S(1)} %dynamic_slice.18, bf16[2048,768]{1,0:T(8,128)(2,1)} %bitcast.74, bf16[768,768]{1,0:T(8,128)(2,1)S(1)} %bitcast.98), kind=kOutput, calls=%fused_computation.4 | convolution fusion | flops 2519728128 | bytes 20057088 | tf_op jit(solution)/shard_map/dot_general | solution.py:747
  183.1 4.0 convolution_convert_fusion.1
  187.1 24.6 %scatter_rows.4 = f32[512,768]{1,0:T(8,128)} custom-call(bf16[4,512,768]{2,1,0:T(8,128)(2,1)} %bitcast.73), custom_call_target="tpu_custom_call" | custom-call | tf_op jit(solution)/shard_map/scatter_rows/pallas_call | solution.py:508
  211.7 2.6 fusion.15
  214.2 1.4 add.146
  215.6 0.8 mul.217
  216.3 0.7 broadcast_multiply_fusion
  218.0 1.0 add_convert_fusion.1
  219.0 0.9 copy-done.4
  219.9 1.1 multiply_reduce_fusion.6
  221.0 1.5 fusion.7
  222.5 1.8 copy.52
  224.3 2.4 multiply_reduce_fusion
  228.0 1.1 copy-done
  229.2 1.7 add_reduce_fusion.1
  230.8 23.3 %gather_rows.4 = bf16[4,512,768]{2,1,0:T(8,128)(2,1)} custom-call(bf16[512,768]{1,0:T(8,128)(2,1)} %get-tuple-element.110.own_ref), custom_call_target="tpu_custom_call" | custom-call | tf_op jit(solution)/shard_map/gather_rows/pallas_call | solution.py:482
  254.2 11.1 %convert_reduce_fusion = (f32[768]{0:T(1024)}, bf16[2048,768]{1,0:T(8,128)(2,1)S(1)}) fusion(f32[2048,768]{1,0:T(8,128)} %get-tuple-element.104, f32[2048,768]{1,0:T(8,128)} %get-tuple-element.117, f32[768]{0:T(1024)S(1)} %copy-done.29, bf16[2048,768]{1,0:T(8,128)(2,1)} %bitcast.77, bf16[768,768]{1,0:T(8,128)(2,1)} %bitcast.100), kind=kOutput, calls=%fused_computation.2 | convolution fusion | flops 2442657024 | bytes 20060160 | tf_op jit(solution)/shard_map/dot_general | solution.py:770
  265.4 4.0 convolution_convert_fusion
  269.4 24.7 %scatter_rows.5 = f32[512,768]{1,0:T(8,128)} custom-call(bf16[4,512,768]{2,1,0:T(8,128)(2,1)} %bitcast.72), custom_call_target="tpu_custom_call" | custom-call | tf_op jit(solution)/shard_map/scatter_rows/pallas_call | solution.py:508
  294.1 2.8 multiply_reduce_fusion.1
  297.6 1.0 add_convert_fusion.2.own_ref
  298.6 23.4 %gather_rows.5 = bf16[4,512,768]{2,1,0:T(8,128)(2,1)} custom-call(bf16[512,768]{1,0:T(8,128)(2,1)} %add_convert_fusion.2.own_ref), custom_call_target="tpu_custom_call" | custom-call | tf_op jit(solution)/shard_map/gather_rows/pallas_call | solution.py:482
  322.0 3.1 convolution_convert_fusion.3
  325.1 1.3 copy.47.dout_ref
  326.4 40.2 %attend_back.1 = bf16[2048,576]{1,0:T(8,128)(2,1)} custom-call(s32[1]{0:T(128)} %copy.63.len_ref, bf16[2048,576]{1,0:T(8,128)(2,1)} %get-tuple-element.33.query_ref.kv_ref, bf16[2048,192]{1,0:T(8,128)(2,1)} %copy.47.dout_ref, f32[2048,192]{1,0:T(8,128)} %get-tuple-element.39.exact_ref, f32[2048,128]{1,0:T(8,128)} %get-tuple-element.40.total_ref, ...), custom_call_target="tpu_custom_call" | custom-call | tf_op jit(solution)/shard_map/attend_back/pallas_call | solution.py:196
  366.6 4.7 convolution_convert_fusion.6
  371.3 1.3 copy.48
  372.6 6.7 %convolution_convert_fusion.5 = bf16[768,768]{1,0:T(8,128)(2,1)} fusion(bf16[2048,768]{1,0:T(8,128)(2,1)} %bitcast.75, bf16[2048,768]{1,0:T(8,128)(2,1)} %copy-done.35), kind=kOutput, calls=%fused_computation.37 | convolution fusion | flops 2416508928 | bytes 7471104 | tf_op jit(solution)/shard_map/dot_general | solution.py:30
  379.3 0.9 convolution_convert_fusion.7
  380.2 0.9 copy.49
  381.1 6.6 %convolution_convert_fusion.4 = bf16[768,768]{1,0:T(8,128)(2,1)} fusion(bf16[2048,768]{1,0:T(8,128)(2,1)} %bitcast.78, bf16[2048,768]{1,0:T(8,128)(2,1)} %copy-done.34), kind=kOutput, calls=%fused_computation.36 | convolution fusion | flops 2416508928 | bytes 7471104 | tf_op jit(solution)/shard_map/dot_general | solution.py:30
  387.7 1.1 convolution_convert_fusion.8
  389.3 2.2 convert_reduce_fusion.1
  392.4 4.6 fusion.19
  397.5 2.7 copy-done.3
  401.2 1.4 copy.50.slots_ref
  402.5 4.8 convert_element_type.127.rows_ref
  407.3 11.1 %leave_slots.1 = bf16[2048,768]{1,0:T(8,128)(2,1)} custom-call(s32[2048,1]{1,0:T(8,128)} %copy.50.slots_ref, bf16[2048,768]{1,0:T(8,128)(2,1)} %convert_element_type.127.rows_ref), custom_call_target="tpu_custom_call" | custom-call | tf_op jit(solution)/shard_map/leave_slots/pallas_call | solution.py:677
  418.4 52.3 %scatter_all.1 = (f32[96,576]{1,0:T(8,128)}, f32[96,768]{1,0:T(8,128)}, f32[96,192]{1,0:T(8,128)}, f32[96,768]{1,0:T(8,128)}, f32[96,128]{1,0:T(8,128)}, /*index=5*/f32[12,96]{1,0:T(8,128)}, f32[512,768]{1,0:T(8,128)}) custom-call(bf16[8,96,576]{2,1,0:T(8,128)(2,1)} %bitcast.71, bf16[8,96,768]{2,1,0:T(8,128)(2,1)} %bitcast.82, bf16[8,96,192]{2,1,0:T(8,128)(2,1)} %bitcast.81, ...), custom_call_target="tpu_custom_call" | custom-call | tf_op jit(solution)/shard_map/scatter_all/pallas_call | solution.py:619
  470.7 1.1 copy.51
  471.9 0.9 copy.53
  472.8 1.6 copy.54
  474.4 1.2 slice.79
  475.6 1.3 slice.80
  478.3 2.7 copy.64
  480.9 0.7 copy.65
  481.6 0.7 copy.66
  (127 shorter events, 14.5 us)
Async XLA Ops:
  66.3 98.0 %copy-start.28 = (f32[768]{0:T(1024)}, f32[768]{0:T(1024)S(1)}, u32[]{:S(2)}) copy-start(f32[768]{0:T(1024)S(1)} %dynamic_slice.18) | copy-start | bytes 9220
  84.1 24.2 %copy-start.6 = (bf16[8,96,192]{2,1,0:T(8,128)(2,1)S(1)}, bf16[8,96,192]{2,1,0:T(8,128)(2,1)}, u32[]{:S(2)}) copy-start(bf16[8,96,192]{2,1,0:T(8,128)(2,1)} %get-tuple-element.35) | copy-start | bytes 884740
  139.1 0.5 copy-start.19
  139.6 24.7 %copy-start.31 = (bf16[8,96,768]{2,1,0:T(8,128)(2,1)S(1)}, bf16[8,96,768]{2,1,0:T(8,128)(2,1)}, u32[]{:S(2)}) copy-start(bf16[8,96,768]{2,1,0:T(8,128)(2,1)} %get-tuple-element.36) | copy-start | bytes 3538948
  164.4 18.7 %copy-start.33 = (bf16[8,96,768]{2,1,0:T(8,128)(2,1)S(1)}, bf16[8,96,768]{2,1,0:T(8,128)(2,1)}, u32[]{:S(2)}) copy-start(bf16[8,96,768]{2,1,0:T(8,128)(2,1)} %get-tuple-element.37) | copy-start | bytes 3538948
  183.1 4.0 copy-start.34
  216.3 3.6 copy-start.8
  216.3 3.6 copy-start.10
  217.1 5.4 %copy-start.13 = (f32[512]{0:T(512)}, f32[512]{0:T(512)S(1)}, u32[]{:S(2)}) copy-start(f32[512]{0:T(512)S(1)} %broadcast_multiply_fusion) | copy-start | bytes 6148
  217.4 0.6 copy-start.21
  218.0 4.6 copy-start.17
  219.0 0.9 copy-start.4
  224.3 3.1 copy-start.14
  224.3 3.1 copy-start.18
  228.0 1.1 copy-start
  229.2 25.0 %copy-start.22 = (f32[512]{0:T(512)}, f32[512]{0:T(512)S(1)}, u32[]{:S(2)}) copy-start(f32[512]{0:T(512)S(1)} %negate_multiply_fusion.2) | copy-start | bytes 6148
  229.2 25.0 %copy-start.29 = (f32[768]{0:T(1024)S(1)}, f32[768]{0:T(1024)}, u32[]{:S(2)}) copy-start(f32[768]{0:T(1024)} %copy-done.28) | copy-start | bytes 9220
  254.2 11.1 %copy-start.32 = (bf16[8,96,768]{2,1,0:T(8,128)(2,1)S(1)}, bf16[8,96,768]{2,1,0:T(8,128)(2,1)}, u32[]{:S(2)}) copy-start(bf16[8,96,768]{2,1,0:T(8,128)(2,1)} %get-tuple-element.36) | copy-start | bytes 3538948
  265.4 4.0 copy-start.35
  269.4 24.7 %copy-start.1 = (f32[512,768]{1,0:T(8,128)S(1)}, f32[512,768]{1,0:T(8,128)}, u32[]{:S(2)}) copy-start(f32[512,768]{1,0:T(8,128)} %copy-done) | copy-start | bytes 4718596
  294.1 2.9 copy-start.20
  372.6 6.7 %copy-start.2 = (bf16[4,512,768]{2,1,0:T(8,128)(2,1)S(1)}, bf16[4,512,768]{2,1,0:T(8,128)(2,1)}, u32[]{:S(2)}) copy-start(bf16[4,512,768]{2,1,0:T(8,128)(2,1)} %gather_rows.5) | copy-start | bytes 9437188
  372.6 6.7 %copy-start.9 = (bf16[2048,192]{1,0:T(8,128)(2,1)S(1)}, bf16[2048,192]{1,0:T(8,128)(2,1)}, u32[]{:S(2)}) copy-start(bf16[2048,192]{1,0:T(8,128)(2,1)} %get-tuple-element.34) | copy-start | bytes 2359300
  381.1 6.7 %copy-start.5 = (bf16[512,768]{1,0:T(8,128)(2,1)S(1)}, bf16[512,768]{1,0:T(8,128)(2,1)}, u32[]{:S(2)}) copy-start(bf16[512,768]{1,0:T(8,128)(2,1)} %copy-done.4) | copy-start | bytes 2359300
  381.1 6.7 %copy-start.7 = (bf16[512,128]{0,1:T(8,128)(2,1)S(1)}, bf16[512,128]{0,1:T(8,128)(2,1)}, u32[]{:S(2)}) copy-start(bf16[512,128]{0,1:T(8,128)(2,1)} %get-tuple-element.111) | copy-start | bytes 393220
  381.1 7.7 %copy-start.30 = (f32[768]{0:T(1024)S(1)}, f32[768]{0:T(1024)}, u32[]{:S(2)}) copy-start(f32[768]{0:T(1024)} %get-tuple-element.94) | copy-start | bytes 9220
  381.1 8.0 %copy-start.27 = (f32[768]{0:T(1024)S(1)}, f32[768]{0:T(1024)}, u32[]{:S(2)}) copy-start(f32[768]{0:T(1024)} %get-tuple-element.80) | copy-start | bytes 9220
  381.1 8.1 %copy-start.25 = (f32[768]{0:T(1024)S(1)}, f32[768]{0:T(1024)}, u32[]{:S(2)}) copy-start(f32[768]{0:T(1024)} %get-tuple-element.78) | copy-start | bytes 9220
  397.0 3.2 copy-start.26
  397.0 3.3 copy-start.24
  397.0 3.3 copy-start.23
  397.0 4.1 copy-start.16
  397.5 2.7 copy-start.3
  470.7 10.2 %copy-start.12 = (f32[96,768]{1,0:T(8,128)S(1)}, f32[96,768]{1,0:T(8,128)}, u32[]{:S(2)}) copy-start(f32[96,768]{1,0:T(8,128)} %get-tuple-element.134) | copy-start | bytes 884740
  470.7 10.9 %copy-start.11 = (f32[96,768]{1,0:T(8,128)S(1)}, f32[96,768]{1,0:T(8,128)}, u32[]{:S(2)}) copy-start(f32[96,768]{1,0:T(8,128)} %get-tuple-element.45) | copy-start | bytes 884740
  470.7 11.6 %copy-start.15 = (f32[96,128]{1,0:T(8,128)S(1)}, f32[96,128]{1,0:T(8,128)}, u32[]{:S(2)}) copy-start(f32[96,128]{1,0:T(8,128)} %get-tuple-element.136) | copy-start | bytes 147460
